TPU v7x, 32 devices: a whole 2x2x4 slice. The times are simulated.
32 devices in a mesh: band: 8 (over z, y), tok: 4 (over x, core).
Axes of the slice: x: 2, y: 2, z: 4, core: 2. Of those that a mesh axis runs over, the one named last changes fastest.
Arguments:
- pixels: bfloat16 [4, 8, 32, 256, 256], P('tok', None, 'band'), may hold values from -6 to 6
- wave_table: float32 [64], replicated, may hold values from 0.4 to 12
- wave_index: int32 [4, 8, 32], P('tok'), may hold values from 0 to 63
- patch_count: int32 [4, 8], P('tok', 'band'), may hold values from 49 to 256, as said below
- d_out: bfloat16 [4, 8, 256, 768], P('tok', 'band'), may hold values from -6 to 6
- gen_w: bfloat16 [196608, 128], P(('band', 'tok')), may hold values from -0.5 to 0.5
- gen_b: float32 [128, 768], replicated, may hold values from -0.25 to 0.25
- bias_token: float32 [128], replicated, may hold values from -6 to 6
- hyper_query: float32 [128, 128], replicated, may hold values from -1 to 1
- hyper_key: float32 [128, 128], replicated, may hold values from -1 to 1
- hyper_value: float32 [128, 128], replicated, may hold values from -0.5 to 0.5
- hyper_out: float32 [128, 128], replicated, may hold values from -0.5 to 0.5
- hyper_up: float32 [128, 2048], replicated, may hold values from -0.5 to 0.5
- hyper_down: float32 [2048, 128], replicated, may hold values from -0.125 to 0.125
- hyper_gain1: float32 [128], replicated, may hold values from 0.1 to 1.9
- hyper_gain2: float32 [128], replicated, may hold values from 0.1 to 1.9
- w_qkv: bfloat16 [768, 2304], P(None, 'tok'), may hold values from -0.21875 to 0.21875
- w_out: bfloat16 [768, 768], P(None, 'tok'), may hold values from -1.75 to 1.75
- w_up: bfloat16 [768, 3072], P(None, 'tok'), may hold values from -0.21875 to 0.21875
- w_down: bfloat16 [3072, 768], P('tok'), may hold values from -0.109375 to 0.109375
- ln1_gain: float32 [768], replicated, may hold values from 0.5 to 1.5
- ln2_gain: float32 [768], replicated, may hold values from 0.5 to 1.5
Outputs:
- layer_out: bfloat16 [4, 8, 256, 768], P('tok', 'band')
- pixel_grad: bfloat16 [4, 8, 32, 256, 256], P('tok', None, 'band')
- grad_gen_w: float32 [196608, 128], P(('band', 'tok'))
- grad_gen_b: float32 [128, 768], replicated
- grad_bias_token: float32 [128], replicated
- grad_hyper_query: float32 [128, 128], replicated
- grad_hyper_key: float32 [128, 128], replicated
- grad_hyper_value: float32 [128, 128], replicated
- grad_hyper_out: float32 [128, 128], replicated
- grad_hyper_up: float32 [128, 2048], replicated
- grad_hyper_down: float32 [2048, 128], replicated
- grad_hyper_gain1: float32 [128], replicated
- grad_hyper_gain2: float32 [128], replicated
- grad_w_qkv: float32 [768, 2304], P(None, ('band', 'tok'))
- grad_w_out: float32 [768, 768], P(None, ('band', 'tok'))
- grad_w_up: float32 [768, 3072], P(None, ('band', 'tok'))
- grad_w_down: float32 [3072, 768], P(('band', 'tok'))
- grad_ln1_gain: float32 [768], P(('band', 'tok'))
- grad_ln2_gain: float32 [768], P(('band', 'tok'))
Inputs may be any that keep to these rules, and one draw needn't show every extreme that they name: `patch_count`: each entry is 49, 196 or 256; every draw has an image with 49 and one with 256.
All inputs are finite; a program needn't handle non-finite values.
Results may differ from a plain program's by a relative error of at most 0.028.
Values may be sent and summed in bfloat16 or wider, within the bound.
A program may use at most 384 MiB of HBM per device.

v0:
```python
import math

import jax
import jax.numpy as jnp
from jax import lax
from jax.sharding import PartitionSpec as P

HD = 64
HHEADS = 4


EPS_BLOCK = 1e-06
EPS_HYPER = 1e-05
PRECISE = lax.Precision.HIGHEST


def layer_norm(values, scaling, epsilon):
    center = values - jnp.mean(values, axis=-1, keepdims=True)
    spread = jnp.mean(center * center, axis=-1, keepdims=True)
    return center * lax.rsqrt(spread + epsilon) * scaling


def block_norm(values, scaling):
    return layer_norm(values, scaling, EPS_BLOCK)


def exact_gelu(values):
    return jax.nn.gelu(values, approximate=False)


def wave_features(lengths, model_dim):
    middle = model_dim // 2
    angular = 1.0 / 10000.0 ** (jnp.arange(middle, dtype=jnp.float32) / middle)
    phases = (100.0 * lengths)[..., None] * angular
    return jnp.concatenate([jnp.sin(phases), jnp.cos(phases)], axis=-1)


def hyper_layer(features, params):
    (
        bias_token,
        hyper_query,
        hyper_key,
        hyper_value,
        hyper_out,
        hyper_up,
        hyper_down,
        hyper_gain1,
        hyper_gain2,
    ) = params
    images = features.shape[0]
    model_dim = features.shape[-1]
    head_size = model_dim // HHEADS
    tokens = jnp.concatenate(
        [features, jnp.broadcast_to(bias_token, (images, 1, model_dim))], axis=1
    )
    length = tokens.shape[1]
    queries = jnp.einsum("nsc,ce->nse", tokens, hyper_query, precision=PRECISE).reshape(
        images, length, HHEADS, head_size
    )
    keys_all = jnp.einsum("nsc,ce->nse", tokens, hyper_key, precision=PRECISE).reshape(
        images, length, HHEADS, head_size
    )
    values_all = jnp.einsum("nsc,ce->nse", tokens, hyper_value, precision=PRECISE).reshape(
        images, length, HHEADS, head_size
    )
    scores = jnp.einsum("nshe,nthe->nhst", queries, keys_all, precision=PRECISE) / math.sqrt(
        head_size
    )
    weights = jax.nn.softmax(scores, axis=-1)
    blended = jnp.einsum("nhst,nthe->nshe", weights, values_all, precision=PRECISE).reshape(
        images, length, model_dim
    )
    segment_one = layer_norm(
        tokens + jnp.einsum("nse,ef->nsf", blended, hyper_out, precision=PRECISE),
        hyper_gain1,
        EPS_HYPER,
    )
    expanded = jax.nn.gelu(
        jnp.einsum("nse,ef->nsf", segment_one, hyper_up, precision=PRECISE), approximate=False
    )
    second = layer_norm(
        segment_one + jnp.einsum("nsf,fe->nse", expanded, hyper_down, precision=PRECISE),
        hyper_gain2,
        EPS_HYPER,
    )
    return (second[:, :-1, :], second[:, -1, :])


def contract_rows(left_side, right_side):
    return lax.dot_general(
        left_side, right_side, (((0,), (0,)), ((), ())), preferred_element_type=jnp.float32
    )


def contract_cols(left_side, right_side):
    return lax.dot_general(
        left_side, right_side, (((1,), (1,)), ((), ())), preferred_element_type=jnp.float32
    )


def attention_scores(queries, keys_low, usable):
    head_size = queries.shape[-1]
    scores = jnp.einsum(
        "iqhe,ikhe->ihqk", queries, keys_low, preferred_element_type=jnp.float32
    ) / math.sqrt(head_size)
    return jnp.where(usable[:, None, None, :], scores, -1e30)


def block_forward(embedded, usable, weights_full, ln1_gain, ln2_gain):
    w_qkv_full, w_out_full, w_up_full, w_down_full = weights_full
    images, slot_count, model_dim = embedded.shape
    row_count = images * slot_count
    head_count = model_dim // HD
    flat_rows = embedded.reshape(row_count, model_dim)
    normed_one = block_norm(flat_rows, ln1_gain).astype(jnp.bfloat16)
    qkv_low = jnp.dot(normed_one, w_qkv_full, preferred_element_type=jnp.float32).astype(
        jnp.bfloat16
    )
    sections = qkv_low.reshape(images, slot_count, 3, head_count, HD)
    queries = sections[:, :, 0]
    keys_low = sections[:, :, 1]
    values_low = sections[:, :, 2]
    scores = attention_scores(queries, keys_low, usable)
    highest = jnp.max(scores, axis=-1, keepdims=True)
    lifted = jnp.exp(scores - highest)
    totals = jnp.sum(lifted, axis=-1, keepdims=True)
    attn_probs = (lifted / totals).astype(jnp.bfloat16)
    log_mass = highest + jnp.log(totals)
    attended = (
        jnp.einsum("ihqk,ikhe->iqhe", attn_probs, values_low, preferred_element_type=jnp.float32)
        .astype(jnp.bfloat16)
        .reshape(row_count, model_dim)
    )
    middle = flat_rows + jnp.dot(attended, w_out_full, preferred_element_type=jnp.float32)
    normed_two = block_norm(middle, ln2_gain).astype(jnp.bfloat16)
    hidden = jnp.dot(normed_two, w_up_full, preferred_element_type=jnp.float32)
    active = exact_gelu(hidden).astype(jnp.bfloat16)
    output = middle + jnp.dot(active, w_down_full, preferred_element_type=jnp.float32)
    return (
        flat_rows,
        normed_one,
        queries,
        keys_low,
        values_low,
        log_mass,
        attended,
        middle,
        normed_two,
        hidden,
        active,
        output,
    )


def block_backward(stored, usable, grad_rows, weights_full, ln1_gain, ln2_gain):
    (
        flat_rows,
        normed_one,
        queries,
        keys_low,
        values_low,
        log_mass,
        attended,
        middle,
        normed_two,
        hidden,
        active,
        output,
    ) = stored
    w_qkv_full, w_out_full, w_up_full, w_down_full = weights_full
    images, slot_count, head_count, head_size = queries.shape
    row_count, model_dim = flat_rows.shape
    grad_low = grad_rows.astype(jnp.bfloat16)
    grad_down = contract_rows(active, grad_low)
    d_active = contract_cols(grad_low, w_down_full)
    gelu_back = jax.vjp(exact_gelu, hidden)[1]
    d_hidden = gelu_back(d_active)[0].astype(jnp.bfloat16)
    grad_up_turned = contract_rows(d_hidden, normed_two)
    d_normed_two = contract_cols(d_hidden, w_up_full)
    norm_back_two = jax.vjp(block_norm, middle, ln2_gain)[1]
    d_middle_norm, grad_gain_two = norm_back_two(d_normed_two)
    d_middle = grad_rows + d_middle_norm
    d_middle_low = d_middle.astype(jnp.bfloat16)
    grad_out_turned = contract_rows(d_middle_low, attended)
    d_attended = (
        contract_cols(d_middle_low, w_out_full)
        .astype(jnp.bfloat16)
        .reshape(images, slot_count, head_count, head_size)
    )
    scores = attention_scores(queries, keys_low, usable)
    attn_float = jnp.exp(scores - log_mass)
    attn_probs = attn_float.astype(jnp.bfloat16)
    d_values = jnp.einsum(
        "ihqk,iqhe->ikhe", attn_probs, d_attended, preferred_element_type=jnp.float32
    ).astype(jnp.bfloat16)
    d_probs = jnp.einsum(
        "iqhe,ikhe->ihqk", d_attended, values_low, preferred_element_type=jnp.float32
    )
    d_scores = (
        attn_float * (d_probs - jnp.sum(attn_float * d_probs, axis=-1, keepdims=True))
    ).astype(jnp.bfloat16)
    d_queries = (
        jnp.einsum("ihqk,ikhe->iqhe", d_scores, keys_low, preferred_element_type=jnp.float32)
        / math.sqrt(head_size)
    ).astype(jnp.bfloat16)
    d_keys = (
        jnp.einsum("ihqk,iqhe->ikhe", d_scores, queries, preferred_element_type=jnp.float32)
        / math.sqrt(head_size)
    ).astype(jnp.bfloat16)
    d_qkv = jnp.stack([d_queries, d_keys, d_values], axis=2).reshape(row_count, 3 * model_dim)
    grad_qkv_turned = contract_rows(d_qkv, normed_one)
    d_normed_one = contract_cols(d_qkv, w_qkv_full)
    norm_back_one = jax.vjp(block_norm, flat_rows, ln1_gain)[1]
    d_flat, grad_gain_one = norm_back_one(d_normed_one)
    return (
        d_middle + d_flat,
        (grad_qkv_turned, grad_out_turned, grad_up_turned, grad_down, grad_gain_one, grad_gain_two),
    )


def body(
    pixels,
    wave_table,
    wave_index,
    patch_count,
    d_out,
    gen_w,
    gen_b,
    bias_token,
    hyper_query,
    hyper_key,
    hyper_value,
    hyper_out,
    hyper_up,
    hyper_down,
    hyper_gain1,
    hyper_gain2,
    w_qkv,
    w_out,
    w_up,
    w_down,
    ln1_gain,
    ln2_gain,
):
    group_images = pixels.shape[1]
    band_share = pixels.shape[2]
    slot_count = pixels.shape[3]
    pixel_count = pixels.shape[4]
    own_images = patch_count.shape[1]
    model_dim = w_out.shape[0]
    hyper_dim = gen_w.shape[1]
    all_bands = wave_index.shape[2]
    factor = 1.0 / math.sqrt(all_bands * pixel_count)
    band_place = lax.axis_index("band")
    hyper_params = (
        bias_token,
        hyper_query,
        hyper_key,
        hyper_value,
        hyper_out,
        hyper_up,
        hyper_down,
        hyper_gain1,
        hyper_gain2,
    )
    catalog = lax.broadcasted_iota(jnp.int32, (1, 1, wave_table.shape[0]), 2)
    picked = (wave_index[0][:, :, None] == catalog).astype(jnp.float32)
    lengths_all = jnp.sum(picked * wave_table, axis=-1)
    weights_full = (
        lax.all_gather(w_qkv, "tok", axis=1, tiled=True),
        lax.all_gather(w_out, "tok", axis=1, tiled=True),
        lax.all_gather(w_up, "tok", axis=1, tiled=True),
        lax.all_gather(w_down, "tok", axis=0, tiled=True),
    )
    hyper_input = wave_features(lengths_all, hyper_dim)

    def run_hyper(params):
        return hyper_layer(hyper_input, params)

    (band_feats, bias_feats), hyper_back = jax.vjp(run_hyper, hyper_params)
    band_low = (
        lax.dynamic_slice_in_dim(band_feats, band_place * band_share, band_share, 1)
        .astype(jnp.bfloat16)
        .reshape(-1, hyper_dim)
    )
    bias_own = lax.dynamic_slice_in_dim(bias_feats, band_place * own_images, own_images, 0)
    gen_full = lax.all_gather(gen_w, ("band", "tok"), axis=0, tiled=True)
    kernels = (contract_cols(band_low, gen_full) * factor).astype(jnp.bfloat16)
    kernel_grid = kernels.reshape(group_images, band_share, pixel_count, model_dim)
    pixel_part = pixels[0]
    product = jnp.einsum(
        "ibsp,ibpd->isd", pixel_part, kernel_grid, preferred_element_type=jnp.float32
    )
    convolved = lax.psum_scatter(
        product.reshape(own_images * slot_count * lax.axis_size("band"), model_dim).astype(
            jnp.bfloat16
        ),
        "band",
        scatter_dimension=0,
        tiled=True,
    ).astype(jnp.float32)
    bias_rows = jnp.dot(bias_own, gen_b, precision=PRECISE)
    embedded = convolved.reshape(own_images, slot_count, model_dim) + bias_rows[:, None, :]
    usable = lax.broadcasted_iota(jnp.int32, (own_images, slot_count), 1) < patch_count[0][:, None]
    stored = block_forward(embedded, usable, weights_full, ln1_gain, ln2_gain)
    row_mask = usable.reshape(-1, 1)
    layer_out = (
        jnp.where(row_mask, stored[-1], 0.0)
        .astype(jnp.bfloat16)
        .reshape(1, own_images, slot_count, model_dim)
    )
    stored = block_forward(
        lax.optimization_barrier(embedded), usable, weights_full, ln1_gain, ln2_gain
    )
    grad_rows = jnp.where(row_mask, d_out[0].reshape(-1, model_dim).astype(jnp.float32), 0.0)
    d_embed, block_terms = block_backward(
        stored, usable, grad_rows, weights_full, ln1_gain, ln2_gain
    )
    d_embed_low = d_embed.astype(jnp.bfloat16).reshape(own_images, slot_count, model_dim)
    d_bias = jnp.sum(d_embed.reshape(own_images, slot_count, model_dim), axis=1)
    d_bias_feat = jnp.dot(d_bias, gen_b.T, precision=PRECISE)
    grad_gen_b = jnp.dot(bias_own.T, d_bias, precision=PRECISE)
    d_gathered = lax.all_gather(d_embed_low, "band", axis=0, tiled=True)
    pixel_grad = jnp.einsum(
        "isd,ibpd->ibsp", d_gathered, kernel_grid, preferred_element_type=jnp.float32
    ).astype(jnp.bfloat16)[None]
    d_kernel = (
        jnp.einsum("ibsp,isd->ibpd", pixels[0], d_gathered, preferred_element_type=jnp.float32)
        .astype(jnp.bfloat16)
        .reshape(-1, pixel_count * model_dim)
    )
    d_band_local = jnp.dot(d_kernel, gen_full, preferred_element_type=jnp.float32) * factor
    grad_gen_w = lax.psum_scatter(
        contract_rows(d_kernel, band_low) * factor, ("band", "tok"), scatter_dimension=0, tiled=True
    )
    d_band_own = d_band_local.reshape(group_images, band_share, hyper_dim)
    d_band = lax.dynamic_update_slice_in_dim(
        jnp.zeros(band_feats.shape, jnp.float32), d_band_own, band_place * band_share, 1
    )
    d_bias_all = lax.dynamic_update_slice_in_dim(
        jnp.zeros(bias_feats.shape, jnp.float32), d_bias_feat, band_place * own_images, 0
    )
    (
        grad_token,
        grad_query,
        grad_key,
        grad_value,
        grad_mix,
        grad_expand,
        grad_shrink,
        grad_first_gain,
        grad_second_gain,
    ) = hyper_back((d_band, d_bias_all))[0]
    qkv_turned, out_turned, up_turned, grad_down, gain_one, gain_two = block_terms
    block_sums = (
        lax.psum_scatter(qkv_turned, ("band", "tok"), scatter_dimension=0, tiled=True),
        lax.psum_scatter(out_turned, ("band", "tok"), scatter_dimension=0, tiled=True),
        lax.psum_scatter(up_turned, ("band", "tok"), scatter_dimension=0, tiled=True),
        lax.psum_scatter(grad_down, ("band", "tok"), scatter_dimension=0, tiled=True),
        lax.psum_scatter(gain_one, ("band", "tok"), scatter_dimension=0, tiled=True),
        lax.psum_scatter(gain_two, ("band", "tok"), scatter_dimension=0, tiled=True),
    )
    hyper_sums = lax.psum(
        (
            grad_token,
            grad_query,
            grad_key,
            grad_value,
            grad_mix,
            grad_expand,
            grad_shrink,
            grad_first_gain,
            grad_second_gain,
            grad_gen_b,
        ),
        ("band", "tok"),
    )
    return (
        layer_out,
        pixel_grad,
        grad_gen_w,
        hyper_sums[9],
        hyper_sums[0],
        hyper_sums[1],
        hyper_sums[2],
        hyper_sums[3],
        hyper_sums[4],
        hyper_sums[5],
        hyper_sums[6],
        hyper_sums[7],
        hyper_sums[8],
        block_sums[0].T,
        block_sums[1].T,
        block_sums[2].T,
        block_sums[3],
        block_sums[4],
        block_sums[5],
    )


def solution(mesh):
    placed = (
        P("tok", None, "band", None, None),
        P(),
        P("tok", None, None),
        P("tok", "band"),
        P("tok", "band", None, None),
        P(("band", "tok"), None),
        P(),
        P(),
        P(),
        P(),
        P(),
        P(),
        P(),
        P(),
        P(),
        P(),
        P(None, "tok"),
        P(None, "tok"),
        P(None, "tok"),
        P("tok", None),
        P(),
        P(),
    )
    return jax.shard_map(
        body,
        mesh=mesh,
        in_specs=placed,
        out_specs=(
            P("tok", "band", None, None),
            P("tok", None, "band", None, None),
            P(("band", "tok"), None),
            P(),
            P(),
            P(),
            P(),
            P(),
            P(),
            P(),
            P(),
            P(),
            P(),
            P(None, ("band", "tok")),
            P(None, ("band", "tok")),
            P(None, ("band", "tok")),
            P(("band", "tok"), None),
            P(("band", "tok")),
            P(("band", "tok")),
        ),
        check_vma=False,
    )
```

profile of v0, /device:TPU:0, one launch (start us, length us, event | category | flops | bytes accessed | tf_op | source)
XLA Modules:
  0.0 2059.1 jit_solution(18307944858478254983)
XLA Ops:
  13.8 1.4 fusion.201
  17.6 3.6 fusion.80
  21.3 6.0 fusion.22
  27.3 2.4 fusion.203
  30.2 259.9 %all-gather.8.cloned.1.call-done = bf16[196608,128]{1,0:T(8,128)(2,1)} async-done(((bf16[6144,128]{1,0:T(8,128)(2,1)}), bf16[196608,128]{1,0:T(8,128)(2,1)}) %all-gather.8.cloned.1.call-update) | async-done | bytes 50331664 | tf_op jit(solution)/shard_map/all_gather | solution.py:287
  290.0 25.9 %fusion.1 = bf16[32,196608]{1,0:T(8,128)(2,1)} fusion(bf16[32,128]{1,0:T(8,128)(2,1)S(1)} %bitcast.310, bf16[196608,128]{1,0:T(8,128)(2,1)} %all-gather.8.cloned.1.call-done), kind=kOutput, calls=%fused_computation.3 | convolution fusion | flops 1623195648 | bytes 62922752 | tf_op jit(solution)/shard_map/dot_general | solution.py:96
  315.9 8.2 copy.211
  324.1 5.7 bitcast_convert_fusion
  333.5 69.1 %reduce-scatter.7.cloned.1.call-done = bf16[256,768]{1,0:T(8,128)(2,1)} async-done(((bf16[2048,768]{1,0:T(8,128)(2,1)}), bf16[256,768]{1,0:T(8,128)(2,1)}) %reduce-scatter.7.cloned.1.call-update) | async-done | bytes 393232 | tf_op jit(solution)/shard_map/reduce_scatter | solution.py:294
  403.8 1.8 fusion.76
  406.0 4.2 convolution_convert_fusion
  410.2 2.9 copy.155
  413.1 1.9 fusion.206
  416.7 1.7 fusion.47
  418.5 2.0 fusion.207
  422.2 5.5 fusion.195
  427.7 29.5 %all-gather.16.cloned.1.call-done = bf16[3072,768]{1,0:T(8,128)(2,1)} async-done(((bf16[768,768]{1,0:T(8,128)(2,1)}), bf16[3072,768]{1,0:T(8,128)(2,1)}) %all-gather.16.cloned.1.call-update) | async-done | bytes 4718608 | tf_op jit(solution)/shard_map/all_gather | solution.py:273
  457.3 10.8 add_convert_fusion
  468.1 2.3 multiply_reduce_fusion.1
  473.1 1.9 copy.157
  475.0 2.8 fusion.62
  478.0 1.8 multiply_reduce_fusion
  483.2 1.9 multiply_reduce_fusion.2
  485.5 1.6 fusion.198
  489.9 1.5 broadcast_multiply_fusion
  491.4 2.9 fusion.208
  494.4 1.4 fusion.68
  495.9 51.9 %all-gather.18.cloned.1.call-done = bf16[2048,768]{1,0:T(8,128)(2,1)} async-done(((bf16[256,768]{1,0:T(8,128)(2,1)}), bf16[2048,768]{1,0:T(8,128)(2,1)}) %all-gather.18.cloned.1.call-update) | async-done | bytes 3145744 | tf_op jit(solution)/shard_map/all_gather | solution.py:323
  547.8 11.1 convert_bitcast_fusion
  558.8 16.8 copy.212
  575.6 23.0 %convolution_multiply_fusion.5 = f32[32,128]{1,0:T(8,128)S(1)} fusion(bf16[32,196608]{1,0:T(8,128)(2,1)} %bitcast.272, bf16[196608,128]{1,0:T(8,128)(2,1)} %all-gather.8.cloned.1.call-done), kind=kOutput, calls=%fused_computation.123 | convolution fusion | flops 1610616832 | bytes 62930944 | tf_op jit(solution)/shard_map/dot_general | solution.py:332
  599.8 4.6 multiply_add_fusion
  604.4 1.5 copy-done.14
  605.8 2.4 multiply_reduce_fusion.12
  609.9 1.3 copy.164
  611.2 2.7 multiply_reduce_fusion.9
  613.9 2.3 convolution_bitcast_fusion.2
  617.1 1.6 convolution_bitcast_fusion.5
  618.8 1.5 fusion.193
  620.3 1.6 convolution_bitcast_fusion.4
  623.9 1.6 convolution_bitcast_fusion.3
  625.6 3.2 convolution_bitcast_fusion.1
  628.8 6.3 convolution_bitcast_fusion
  635.2 5.4 fusion.87
  641.6 11.6 fusion.34
  653.9 6.6 fusion.194
  661.3 39.6 %convolution_multiply_fusion = f32[196608,128]{1,0:T(8,128)} fusion(bf16[32,196608]{1,0:T(8,128)(2,1)} %bitcast.273, bf16[32,128]{1,0:T(8,128)(2,1)S(1)} %bitcast.311), kind=kOutput, calls=%fused_computation.1 | convolution fusion | flops 1635778560 | bytes 113254400 | tf_op jit(solution)/shard_map/dot_general | solution.py:90
  701.9 3.2 convolution_convert_fusion.1
  706.7 1.4 fusion.204
  710.2 13.5 fusion.65
  723.7 11.1 convert_bitcast_fusion.1
  734.9 6.6 copy.179
  745.3 39.6 %all-reduce.4 = (f32[128]{0:T(128)}, f32[128]{0:T(128)}, f32[128]{0:T(128)}, f32[768]{0:T(1024)S(1)}, f32[768]{0:T(1024)S(1)}) all-reduce(f32[128]{0:T(128)S(1)} %fusion.148, f32[128]{0:T(128)S(1)} %copy-done.107, f32[128]{0:T(128)S(1)} %copy-done.106, f32[768]{0:T(1024)S(1)} %copy-done.105, ...), channel_id=1, replica_groups=mesh['band'=8,'tok'=4] {'band','tok'}, use_global_device_ids=true, to_apply=%region_34.35 | all-reduce | flops 1920 | bytes 15360 | tf_op jit(solution)/shard_map/psum | solution.py:363
  786.1 12.8 all-reduce.8.cloned.1.call-done
  798.9 124.6 %reduce-scatter.11.cloned.1.call-done = f32[72,768]{1,0:T(8,128)} async-done(((f32[2304,768]{1,0:T(8,128)}), f32[72,768]{1,0:T(8,128)}) %reduce-scatter.11.cloned.1.call-update) | async-done | bytes 221200 | tf_op jit(solution)/shard_map/reduce_scatter | solution.py:356
  923.5 142.3 %reduce-scatter.17.cloned.1.call-done = f32[96,768]{1,0:T(8,128)} async-done(((f32[3072,768]{1,0:T(8,128)}), f32[96,768]{1,0:T(8,128)}) %reduce-scatter.17.cloned.1.call-update) | async-done | bytes 294928 | tf_op jit(solution)/shard_map/reduce_scatter | solution.py:359
  1065.8 141.0 %reduce-scatter.15.cloned.1.call-done = f32[96,768]{1,0:T(8,128)} async-done(((f32[3072,768]{1,0:T(8,128)}), f32[96,768]{1,0:T(8,128)}) %reduce-scatter.15.cloned.1.call-update) | async-done | bytes 294928 | tf_op jit(solution)/shard_map/reduce_scatter | solution.py:358
  1206.8 833.8 %reduce-scatter.9.cloned.1.call-done = f32[6144,128]{1,0:T(8,128)} async-done(((f32[196608,128]{1,0:T(8,128)}), f32[6144,128]{1,0:T(8,128)}) %reduce-scatter.9.cloned.1.call-update) | async-done | bytes 3145744 | tf_op jit(solution)/shard_map/reduce_scatter | solution.py:333
  2040.6 1.8 copy.232
  2042.4 1.5 copy.233
  2043.8 1.5 copy.234
  2045.3 1.5 copy.235
  2046.8 1.5 copy.236
  2048.3 2.3 copy.237
  (333 shorter events, 44.1 us)
Async XLA Ops:
  8.0 9.6 copy-start
  8.1 5.1 copy-start.50
  8.1 282.0 %all-gather.8.cloned.1.call-start = ((), (), s32[]{:S(2)}) async-start(), calls=%async_computation.6 | async-start | bytes 51904512 | tf_op jit(solution)/shard_map/all_gather | solution.py:287
  8.8 393.8 %reduce-scatter.7.cloned.1.call-start = ((), (), s32[]{:S(2)}) async-start(), calls=%async_computation.7 | async-start | bytes 3538944 | tf_op jit(solution)/shard_map/reduce_scatter | solution.py:294
  13.8 7.5 copy-start.27
  15.4 5.9 copy-start.63
  21.3 8.4 copy-start.4
  21.3 6.0 copy-start.47
  29.9 286.0 %copy-start.67 = (f32[8,33]{1,0:T(8,128)}, f32[8,33]{1,0:T(8,128)S(1)}, u32[]{:S(2)}) copy-start(f32[8,33]{1,0:T(8,128)S(1)} %multiply_reduce_fusion.14) | copy-start | bytes 3172
  30.2 285.8 %copy-start.57 = (bf16[8,4,128]{2,1,0:T(4,128)(2,1)}, bf16[8,4,128]{2,1,0:T(4,128)(2,1)S(1)}, u32[]{:S(2)}) copy-start(bf16[8,4,128]{2,1,0:T(4,128)(2,1)S(1)} %dynamic-slice_convert_fusion) | copy-start | bytes 24580
  315.9 8.2 copy-start.10
  324.1 5.8 copy-start.11
  329.9 76.1 %all-gather.10.cloned.1.call-start = ((), (), s32[]{:S(2)}) async-start(), calls=%async_computation.8 | async-start | bytes 4423680 | tf_op jit(solution)/shard_map/all_gather | solution.py:270
  330.5 75.6 %copy-start.69 = (f32[768]{0:T(1024)S(1)}, f32[768]{0:T(1024)}, u32[]{:S(2)}) copy-start(f32[768]{0:T(1024)} %param.42) | copy-start | bytes 9220
  330.5 88.0 %all-gather.12.cloned.1.call-start = ((), (), s32[]{:S(2)}) async-start(), calls=%async_computation.9 | async-start | bytes 1474560 | tf_op jit(solution)/shard_map/all_gather | solution.py:271
  331.1 91.2 %all-gather.14.cloned.1.call-start = ((), (), s32[]{:S(2)}) async-start(), calls=%async_computation.10 | async-start | bytes 5898240 | tf_op jit(solution)/shard_map/all_gather | solution.py:272
  331.6 125.6 %all-gather.16.cloned.1.call-start = ((), (), s32[]{:S(2)}) async-start(), calls=%async_computation.11 | async-start | bytes 5898240 | tf_op jit(solution)/shard_map/all_gather | solution.py:273
  332.4 215.4 %all-gather.18.cloned.1.call-start = ((), (), s32[]{:S(2)}) async-start(), calls=%async_computation.17 | async-start | bytes 3538944 | tf_op jit(solution)/shard_map/all_gather | solution.py:323
  332.4 73.2 %copy-start.94 = (f32[8,1,128]{2,1,0:T(1,128)}, f32[8,1,128]{2,1,0:T(1,128)S(1)}, u32[]{:S(2)}) copy-start(f32[8,1,128]{2,1,0:T(1,128)S(1)} %slice.33) | copy-start | bytes 12292
  333.1 80.0 %copy-start.95 = (pred[256]{0:T(512)(128)(4,1)}, pred[256]{0:T(512)(128)(4,1)S(1)}, u32[]{:S(2)}) copy-start(pred[256]{0:T(512)(128)(4,1)S(1)} %iota_compare_fusion.1) | copy-start | bytes 772
  333.5 76.8 %copy-start.59 = (f32[768]{0:T(1024)}, f32[768]{0:T(1024)S(1)}, u32[]{:S(2)}) copy-start(f32[768]{0:T(1024)S(1)} %convolution_reduce_fusion) | copy-start | bytes 9220
  406.0 7.2 copy-start.87
  406.0 7.1 copy-start.91
  418.4 9.3 copy-start.39
  457.3 10.8 copy-start.72
  457.3 10.8 copy-start.75
  457.3 10.8 copy-start.83
  457.3 10.8 copy-start.108
  487.1 299.0 %reduce-scatter.13.cloned.1.call-start = ((), (), s32[]{:S(2)}) async-start(), calls=%async_computation.14 | async-start | bytes 2433024 | tf_op jit(solution)/shard_map/reduce_scatter | solution.py:357
  494.3 304.5 %all-reduce.8.cloned.1.call-start = ((), (), s32[]{:S(2)}) async-start(), calls=%async_computation.18 | async-start | bytes 5505024 | tf_op jit(solution)/shard_map/psum | solution.py:363
  575.6 23.1 %copy-start.100 = (f32[128]{0:T(128)S(1)}, f32[128]{0:T(128)}, u32[]{:S(2)}) copy-start(f32[128]{0:T(128)} %param.37) | copy-start | bytes 1540
  575.6 23.8 %copy-start.68 = (f32[8,33]{1,0:T(8,128)S(1)}, f32[8,33]{1,0:T(8,128)}, u32[]{:S(2)}) copy-start(f32[8,33]{1,0:T(8,128)} %copy-done.67) | copy-start | bytes 3172
  575.6 24.1 %copy-start.5 = (f32[8,33,2048]{2,1,0:T(8,128)S(1)}, f32[8,33,2048]{2,1,0:T(8,128)}, u32[]{:S(2)}) copy-start(f32[8,33,2048]{2,1,0:T(8,128)} %copy-done.4) | copy-start | bytes 6488068
  575.6 24.1 %copy-start.8 = (f32[8,33,2048]{2,1,0:T(8,128)S(1)}, f32[8,33,2048]{2,1,0:T(8,128)}, u32[]{:S(2)}) copy-start(f32[8,33,2048]{2,1,0:T(8,128)} %copy-done.7) | copy-start | bytes 6488068
  599.7 6.1 copy-start.81
  608.2 8.0 copy-start.64
  609.2 7.9 copy-start.45
  611.2 7.6 copy-start.28
  616.2 5.7 copy-start.37
  617.1 6.0 copy-start.31
  618.8 6.8 copy-start.15
  618.8 6.8 copy-start.82
  621.9 6.9 copy-start.6
  621.9 6.9 copy-start.9
  621.9 6.9 copy-start.44
  628.8 6.4 copy-start.71
  628.8 6.4 copy-start.79
  628.8 6.4 copy-start.93
  635.1 288.3 %reduce-scatter.11.cloned.1.call-start = ((), (), s32[]{:S(2)}) async-start(), calls=%async_computation.13 | async-start | bytes 7299072 | tf_op jit(solution)/shard_map/reduce_scatter | solution.py:356
  640.6 425.2 %reduce-scatter.17.cloned.1.call-start = ((), (), s32[]{:S(2)}) async-start(), calls=%async_computation.16 | async-start | bytes 9732096 | tf_op jit(solution)/shard_map/reduce_scatter | solution.py:359
  653.2 553.6 %reduce-scatter.15.cloned.1.call-start = ((), (), s32[]{:S(2)}) async-start(), calls=%async_computation.15 | async-start | bytes 9732096 | tf_op jit(solution)/shard_map/reduce_scatter | solution.py:358
  660.6 1380.0 %reduce-scatter.9.cloned.1.call-start = ((), (), s32[]{:S(2)}) async-start(), calls=%async_computation.12 | async-start | bytes 103809024 | tf_op jit(solution)/shard_map/reduce_scatter | solution.py:333
  734.8 6.6 copy-start.32
  734.8 6.6 copy-start.51
  734.8 7.6 copy-start.34
  734.8 7.6 copy-start.53
  734.9 8.6 copy-start.36
  734.9 8.6 copy-start.54
  734.9 10.4 copy-start.104
  734.9 10.4 copy-start.105
  734.9 10.4 copy-start.106
  734.9 10.4 copy-start.107
  742.5 1309.1 %copy-start.1 = (f32[128,2048]{1,0:T(8,128)S(1)}, f32[128,2048]{1,0:T(8,128)}, u32[]{:S(2)}) copy-start(f32[128,2048]{1,0:T(8,128)} %param.34) | copy-start | bytes 3145732
  798.9 1251.7 %copy-start.46 = (f32[2048,128]{1,0:T(8,128)S(1)}, f32[2048,128]{1,0:T(8,128)}, u32[]{:S(2)}) copy-start(f32[2048,128]{1,0:T(8,128)} %get-tuple-element.165) | copy-start | bytes 3145732
  (59 other events, 135.8 us)
Sparse Core Ops, SparseCore 0:
  11.8 278.2 all-gather.7
  330.0 72.5 reduce-scatter.6
  487.3 60.4 all-gather.17
  553.5 97.6 reduce-scatter.12
  659.7 139.0 all-reduce.7
  805.0 118.4 reduce-scatter.10
  931.0 134.7 reduce-scatter.16
  1072.3 134.5 reduce-scatter.14
  1215.0 825.6 reduce-scatter.8
Sparse Core Ops, SparseCore 1:
  331.9 28.7 all-gather.9
  362.2 17.3 all-gather.11
  381.0 37.3 all-gather.13
  419.9 37.3 all-gather.15
where the time goes:
time: 2070 us; the launch traced here: 2060 us
  waiting for transfers between devices  1670 us (81%)
  matrix products  245 us (12%)
  local copies, waits for them, and re-layouts  65.3 us (3%)
  blocking collectives  39.6 us (2%)
  other arithmetic  22.8 us (1%)
    reduce_scatter x1, waiting for transfers between devices, body(): lax.psum_scatter(contract_rows(d_kernel, band_low) * factor, ('band', 'to...  834 us
    all_gather x1, waiting for transfers between devices, body(): gen_full = lax.all_gather(gen_w, ('band', 'tok'), axis=0, tiled=True)  260 us
    reduce_scatter x1, waiting for transfers between devices, body(): lax.psum_scatter(grad_down, ('band', 'tok'), scatter_dimension=0, tiled=T...  142 us
    reduce_scatter x1, waiting for transfers between devices, body(): lax.psum_scatter(up_turned, ('band', 'tok'), scatter_dimension=0, tiled=T...  141 us
    reduce_scatter x1, waiting for transfers between devices, body(): lax.psum_scatter(qkv_turned, ('band', 'tok'), scatter_dimension=0, tiled=...  125 us
    reduce_scatter x1, waiting for transfers between devices, body(): lax.psum_scatter(product.reshape(own_images * slot_count * lax.axis_size(...  69.1 us
    dot_general x5, matrix products, contract_rows(): lax.dot_general(left_side, right_side, (((0,), (0,)), ((), ())), preferre...  66.2 us
    unnamed x232, local copies, waits for them, and re-layouts  54.6 us
  transfers between devices with their start and end apart: 13, of which 9 were waited for; matrix products, arithmetic and copies ran while one was open for 12% of the time, Pallas kernels for 0%

commit v1 on v0

--- a/solution.py
+++ b/solution.py
@@ -242,14 +242,13 @@
     ln1_gain,
     ln2_gain,
 ):
-    group_images = pixels.shape[1]
-    band_share = pixels.shape[2]
-    slot_count = pixels.shape[3]
-    pixel_count = pixels.shape[4]
+    group_images, band_share, slot_count, pixel_count = pixels.shape[1:]
     own_images = patch_count.shape[1]
     model_dim = w_out.shape[0]
     hyper_dim = gen_w.shape[1]
     all_bands = wave_index.shape[2]
+    owners = lax.axis_size("band")
+    slice_pixels = pixel_count // owners
     factor = 1.0 / math.sqrt(all_bands * pixel_count)
     band_place = lax.axis_index("band")
     hyper_params = (
@@ -263,38 +262,45 @@
         hyper_gain1,
         hyper_gain2,
     )
-    catalog = lax.broadcasted_iota(jnp.int32, (1, 1, wave_table.shape[0]), 2)
-    picked = (wave_index[0][:, :, None] == catalog).astype(jnp.float32)
-    lengths_all = jnp.sum(picked * wave_table, axis=-1)
+    pixel_turned = pixels[0].reshape(
+        group_images, band_share, slot_count, owners, slice_pixels
+    ).transpose(3, 0, 4, 1, 2)
+    pixel_slices = lax.all_to_all(pixel_turned, "band", 0, 0, tiled=True)
+    pixel_slices = pixel_slices.transpose(1, 2, 0, 3, 4).reshape(
+        group_images, slice_pixels * all_bands, slot_count
+    )
+    gen_part = lax.all_gather(gen_w, "tok", axis=0, tiled=True)
+    gen_grid = gen_part.reshape(slice_pixels, model_dim, hyper_dim)
     weights_full = (
         lax.all_gather(w_qkv, "tok", axis=1, tiled=True),
         lax.all_gather(w_out, "tok", axis=1, tiled=True),
         lax.all_gather(w_up, "tok", axis=1, tiled=True),
         lax.all_gather(w_down, "tok", axis=0, tiled=True),
     )
+    catalog = lax.broadcasted_iota(jnp.int32, (1, 1, wave_table.shape[0]), 2)
+    picked = (wave_index[0][:, :, None] == catalog).astype(jnp.float32)
+    lengths_all = jnp.sum(picked * wave_table, axis=-1)
     hyper_input = wave_features(lengths_all, hyper_dim)
+    band_feats = hyper_layer(hyper_input, hyper_params)[0]
+    band_low = band_feats.astype(jnp.bfloat16).reshape(-1, hyper_dim)
+    own_input = lax.dynamic_slice_in_dim(hyper_input, band_place * own_images, own_images, 0)
 
     def run_hyper(params):
-        return hyper_layer(hyper_input, params)
-
-    (band_feats, bias_feats), hyper_back = jax.vjp(run_hyper, hyper_params)
-    band_low = (
-        lax.dynamic_slice_in_dim(band_feats, band_place * band_share, band_share, 1)
-        .astype(jnp.bfloat16)
-        .reshape(-1, hyper_dim)
-    )
-    bias_own = lax.dynamic_slice_in_dim(bias_feats, band_place * own_images, own_images, 0)
-    gen_full = lax.all_gather(gen_w, ("band", "tok"), axis=0, tiled=True)
-    kernels = (contract_cols(band_low, gen_full) * factor).astype(jnp.bfloat16)
-    kernel_grid = kernels.reshape(group_images, band_share, pixel_count, model_dim)
-    pixel_part = pixels[0]
+        return hyper_layer(own_input, params)
+
+    (_, bias_own), hyper_back = jax.vjp(run_hyper, hyper_params)
+    kernels = (
+        jnp.einsum("pdc,nc->pnd", gen_grid, band_low, preferred_element_type=jnp.float32) * factor
+    ).astype(jnp.bfloat16)
+    kernel_grid = kernels.reshape(slice_pixels, group_images, all_bands, model_dim)
+    kernel_rows = kernel_grid.transpose(1, 0, 2, 3).reshape(
+        group_images, slice_pixels * all_bands, model_dim
+    )
     product = jnp.einsum(
-        "ibsp,ibpd->isd", pixel_part, kernel_grid, preferred_element_type=jnp.float32
+        "iks,ikd->isd", pixel_slices, kernel_rows, preferred_element_type=jnp.float32
     )
     convolved = lax.psum_scatter(
-        product.reshape(own_images * slot_count * lax.axis_size("band"), model_dim).astype(
-            jnp.bfloat16
-        ),
+        product.reshape(group_images * slot_count, model_dim).astype(jnp.bfloat16),
         "band",
         scatter_dimension=0,
         tiled=True,
@@ -309,9 +315,6 @@
         .astype(jnp.bfloat16)
         .reshape(1, own_images, slot_count, model_dim)
     )
-    stored = block_forward(
-        lax.optimization_barrier(embedded), usable, weights_full, ln1_gain, ln2_gain
-    )
     grad_rows = jnp.where(row_mask, d_out[0].reshape(-1, model_dim).astype(jnp.float32), 0.0)
     d_embed, block_terms = block_backward(
         stored, usable, grad_rows, weights_full, ln1_gain, ln2_gain
@@ -321,25 +324,35 @@
     d_bias_feat = jnp.dot(d_bias, gen_b.T, precision=PRECISE)
     grad_gen_b = jnp.dot(bias_own.T, d_bias, precision=PRECISE)
     d_gathered = lax.all_gather(d_embed_low, "band", axis=0, tiled=True)
-    pixel_grad = jnp.einsum(
-        "isd,ibpd->ibsp", d_gathered, kernel_grid, preferred_element_type=jnp.float32
-    ).astype(jnp.bfloat16)[None]
+    grad_slices = jnp.einsum(
+        "ikd,isd->iks", kernel_rows, d_gathered, preferred_element_type=jnp.float32
+    ).astype(jnp.bfloat16)
+    grad_slices = grad_slices.reshape(
+        group_images, slice_pixels, owners, band_share, slot_count
+    ).transpose(2, 0, 1, 3, 4)
+    grad_slices = lax.all_to_all(grad_slices, "band", 0, 0, tiled=True)
+    pixel_grad = grad_slices.transpose(1, 3, 4, 0, 2).reshape(pixels.shape)
+    d_kernel = jnp.einsum(
+        "iks,isd->ikd", pixel_slices, d_gathered, preferred_element_type=jnp.float32
+    ).astype(jnp.bfloat16)
     d_kernel = (
-        jnp.einsum("ibsp,isd->ibpd", pixels[0], d_gathered, preferred_element_type=jnp.float32)
-        .astype(jnp.bfloat16)
-        .reshape(-1, pixel_count * model_dim)
-    )
-    d_band_local = jnp.dot(d_kernel, gen_full, preferred_element_type=jnp.float32) * factor
+        d_kernel.reshape(group_images, slice_pixels, all_bands, model_dim)
+        .transpose(1, 0, 2, 3)
+        .reshape(slice_pixels, group_images * all_bands, model_dim)
+    )
+    d_band_part = (
+        jnp.einsum("pnd,pdc->nc", d_kernel, gen_grid, preferred_element_type=jnp.float32) * factor
+    )
+    d_band_own = lax.psum_scatter(d_band_part, "band", scatter_dimension=0, tiled=True)
+    gen_part_grad = (
+        jnp.einsum("pnd,nc->pdc", d_kernel, band_low, preferred_element_type=jnp.float32) * factor
+    )
     grad_gen_w = lax.psum_scatter(
-        contract_rows(d_kernel, band_low) * factor, ("band", "tok"), scatter_dimension=0, tiled=True
-    )
-    d_band_own = d_band_local.reshape(group_images, band_share, hyper_dim)
-    d_band = lax.dynamic_update_slice_in_dim(
-        jnp.zeros(band_feats.shape, jnp.float32), d_band_own, band_place * band_share, 1
-    )
-    d_bias_all = lax.dynamic_update_slice_in_dim(
-        jnp.zeros(bias_feats.shape, jnp.float32), d_bias_feat, band_place * own_images, 0
-    )
+        gen_part_grad.reshape(-1, hyper_dim).astype(jnp.bfloat16),
+        "tok",
+        scatter_dimension=0,
+        tiled=True,
+    ).astype(jnp.float32)
     (
         grad_token,
         grad_query,
@@ -350,13 +363,19 @@
         grad_shrink,
         grad_first_gain,
         grad_second_gain,
-    ) = hyper_back((d_band, d_bias_all))[0]
+    ) = hyper_back((d_band_own.reshape(own_images, all_bands, hyper_dim), d_bias_feat))[0]
     qkv_turned, out_turned, up_turned, grad_down, gain_one, gain_two = block_terms
+
+    def spread(term):
+        return lax.psum_scatter(
+            term.astype(jnp.bfloat16), ("band", "tok"), scatter_dimension=0, tiled=True
+        ).astype(jnp.float32)
+
     block_sums = (
-        lax.psum_scatter(qkv_turned, ("band", "tok"), scatter_dimension=0, tiled=True),
-        lax.psum_scatter(out_turned, ("band", "tok"), scatter_dimension=0, tiled=True),
-        lax.psum_scatter(up_turned, ("band", "tok"), scatter_dimension=0, tiled=True),
-        lax.psum_scatter(grad_down, ("band", "tok"), scatter_dimension=0, tiled=True),
+        spread(qkv_turned),
+        spread(out_turned),
+        spread(up_turned),
+        spread(grad_down),
         lax.psum_scatter(gain_one, ("band", "tok"), scatter_dimension=0, tiled=True),
         lax.psum_scatter(gain_two, ("band", "tok"), scatter_dimension=0, tiled=True),
     )

time: 2070 us -> 1240 us (0.60)
  waiting for transfers between devices: 1670 us -> 875 us
  matrix products: 245 us -> 151 us
  local copies, waits for them, and re-layouts: 65.3 us -> 104 us
    reduce_scatter x6 -> x7, waiting for transfers between devices: 1310 us -> 494 us  [the longest x4 382 us: spread(): lax.psum_scatter(term.astype(jnp.bfloat16), ('band', 'tok'), scatter_dime...]
    all_gather x1, waiting for transfers between devices: 260 us -> 0.01 us  [body(): gen_part = lax.all_gather(gen_w, 'tok', axis=0, tiled=True)]
    psum x1, waiting for transfers between devices: 12.8 us -> 145 us  [body(): lax.psum((grad_token, grad_query, grad_key, grad_value, grad_mix, grad_ex...]
    all_to_all x0 -> x2, waiting for transfers between devices: none -> 70.8 us  [the longest x1 70.8 us: body(): pixel_slices = lax.all_to_all(pixel_turned, 'band', 0, 0, tiled=True)]
    dot_general x5 -> x4, matrix products: 66.2 us -> 13 us  [contract_rows(): lax.dot_general(left_side, right_side, (((0,), (0,)), ((), ())), preferre...]
    all_gather x1, waiting for transfers between devices: 0.03 us -> 36.6 us  [body(): lax.all_gather(w_up, 'tok', axis=1, tiled=True)]
    dot_general x5 -> x4, matrix products: 42.1 us -> 10.4 us  [contract_cols(): lax.dot_general(left_side, right_side, (((1,), (1,)), ((), ())), preferre...]
    all_gather x1, waiting for transfers between devices: 0.03 us -> 29.1 us  [body(): lax.all_gather(w_qkv, 'tok', axis=1, tiled=True)]
  transfers between devices with their start and end apart: 13 -> 16, of which waited for: 9 -> 13; matrix products, arithmetic and copies ran while one was open for 12% -> 14% of each run, Pallas kernels for 0% -> 0%
where the time goes in v1:
time: 1240 us; the launch traced here: 1230 us
  waiting for transfers between devices  875 us (71%)
  matrix products  151 us (12%)
  local copies, waits for them, and re-layouts  104 us (8%)
  blocking collectives  40.1 us (3%)
  other arithmetic  27.4 us (2%)
  between operations  16.6 us (1%)
  starting transfers between devices  13.5 us (1%)
    reduce_scatter x4, waiting for transfers between devices, spread(): lax.psum_scatter(term.astype(jnp.bfloat16), ('band', 'tok'), scatter_dime...  382 us
    psum x1, waiting for transfers between devices, body(): lax.psum((grad_token, grad_query, grad_key, grad_value, grad_mix, grad_ex...  145 us
    all_to_all x1, waiting for transfers between devices, body(): pixel_slices = lax.all_to_all(pixel_turned, 'band', 0, 0, tiled=True)  70.8 us
    reduce_scatter x1, waiting for transfers between devices, body(): lax.psum_scatter(product.reshape(group_images * slot_count, model_dim).as...  64.9 us
    all_gather x1, waiting for transfers between devices, body(): d_gathered = lax.all_gather(d_embed_low, 'band', axis=0, tiled=True)  60.4 us
    reduce_scatter x1, waiting for transfers between devices, body(): lax.psum_scatter(gen_part_grad.reshape(-1, hyper_dim).astype(jnp.bfloat16...  46.7 us
    psum x1, blocking collectives, body(): lax.psum((grad_token, grad_query, grad_key, grad_value, grad_mix, grad_ex...  40.1 us
    all_gather x1, waiting for transfers between devices, body(): lax.all_gather(w_up, 'tok', axis=1, tiled=True)  36.6 us
  transfers between devices with their start and end apart: 16, of which 13 were waited for; matrix products, arithmetic and copies ran while one was open for 14% of the time, Pallas kernels for 0%

profile of v1, /device:TPU:0, one launch (start us, length us, event | category | flops | bytes accessed | tf_op | source)
XLA Modules:
  0.0 1227.8 jit_solution(10499054923508806669)
XLA Ops:
  7.9 6.4 copy.172
  14.4 4.9 copy.173
  19.3 7.4 all-to-all-start
  33.2 3.6 fusion.135
  38.5 10.3 fusion.271
  49.1 70.8 %all-to-all-done = bf16[8,8,32,4,256]{4,2,3,1,0:T(8,128)(2,1)} async-done(((bf16[8,8,32,4,256]{4,2,3,1,0:T(8,128)(2,1)}), bf16[8,8,32,4,256]{4,2,3,1,0:T(8,128)(2,1)}, u32[]{:S(2)}, u32[]{:S(2)}) %all-to-all-start) | async-done | bytes 4194336 | tf_op jit(solution)/shard_map/all_to_all | solution.py:268
  120.0 6.6 copy.174
  126.6 9.2 multiply_convert_fusion
  135.7 11.2 copy.171
  147.0 10.0 fusion.68
  165.7 64.9 %reduce-scatter.8.cloned.1.call-done = bf16[256,768]{1,0:T(8,128)(2,1)} async-done(((bf16[2048,768]{1,0:T(8,128)(2,1)}), bf16[256,768]{1,0:T(8,128)(2,1)}) %reduce-scatter.8.cloned.1.call-update) | async-done | bytes 393232 | tf_op jit(solution)/shard_map/reduce_scatter | solution.py:302
  233.0 29.1 %all-gather.10.cloned.1.call-done = bf16[768,2304]{0,1:T(8,128)(2,1)} async-done(((bf16[768,576]{0,1:T(8,128)(2,1)}), bf16[768,2304]{0,1:T(8,128)(2,1)}) %all-gather.10.cloned.1.call-update) | async-done | bytes 3538960 | tf_op jit(solution)/shard_map/all_gather | solution.py:275
  262.1 4.3 convolution_convert_fusion.3
  266.4 1.6 copy.180
  270.4 1.4 fusion.105
  271.9 9.1 all-gather.12.cloned.1.call-done
  281.0 2.0 fusion.276
  283.3 36.6 %all-gather.14.cloned.1.call-done = bf16[768,3072]{1,0:T(8,128)(2,1)} async-done(((bf16[768,768]{1,0:T(8,128)(2,1)}), bf16[768,3072]{1,0:T(8,128)(2,1)}) %all-gather.14.cloned.1.call-update) | async-done | bytes 4718608 | tf_op jit(solution)/shard_map/all_gather | solution.py:277
  319.9 11.9 multiply_convert_fusion.2
  331.7 27.0 %all-gather.16.cloned.1.call-done = bf16[3072,768]{1,0:T(8,128)(2,1)} async-done(((bf16[768,768]{1,0:T(8,128)(2,1)}), bf16[3072,768]{1,0:T(8,128)(2,1)}) %all-gather.16.cloned.1.call-update) | async-done | bytes 4718608 | tf_op jit(solution)/shard_map/all_gather | solution.py:278
  358.8 6.4 add_convert_fusion
  365.3 2.2 multiply_reduce_fusion.1
  370.3 2.6 fusion.115
  379.1 1.8 fusion.266
  381.1 60.4 %all-gather.18.cloned.1.call-done = bf16[2048,768]{1,0:T(8,128)(2,1)} async-done(((bf16[256,768]{1,0:T(8,128)(2,1)}), bf16[2048,768]{1,0:T(8,128)(2,1)}) %all-gather.18.cloned.1.call-update) | async-done | bytes 3145744 | tf_op jit(solution)/shard_map/all_gather | solution.py:326
  441.5 11.6 convert_bitcast_fusion
  453.1 16.9 %copy.190 = bf16[8,1024,768]{2,1,0:T(8,128)(2,1)} copy(bf16[8,1024,768]{1,2,0:T(8,128)(2,1)} %convert_bitcast_fusion) | data formatting | bytes 25165824 | tf_op jit(solution)/shard_map/convert_element_type | solution.py:337
  470.0 6.8 copy.191
  476.8 4.4 fusion.121
  481.3 2.8 convolution_convert_fusion.5
  484.2 2.9 convolution_convert_fusion.2
  488.7 3.6 convolution_convert_fusion
  494.0 3.7 convolution_convert_fusion.1
  498.5 10.8 fusion
  509.4 11.0 convolution_convert_fusion.4
  520.3 6.9 reshape.726
  527.3 8.8 copy.228
  536.0 4.7 all-to-all-start.1
  543.7 1.9 convolution_bitcast_fusion.6
  545.6 1.5 broadcast_multiply_fusion
  547.3 1.5 fusion.175
  551.8 2.5 fusion.176
  559.6 2.1 fusion.202
  561.7 2.8 fusion.154
  564.6 4.5 fusion.112
  569.1 101.1 %reduce-scatter.16.cloned.1.call-done = bf16[24,768]{1,0:T(8,128)(2,1)} async-done(((bf16[768,768]{1,0:T(8,128)(2,1)}), bf16[24,768]{1,0:T(8,128)(2,1)}) %reduce-scatter.16.cloned.1.call-update) | async-done | bytes 36880 | tf_op jit(solution)/shard_map/reduce_scatter | solution.py:370
  671.7 105.8 %reduce-scatter.14.cloned.1.call-done = bf16[72,768]{1,0:T(8,128)(2,1)} async-done(((bf16[2304,768]{1,0:T(8,128)(2,1)}), bf16[72,768]{1,0:T(8,128)(2,1)}) %reduce-scatter.14.cloned.1.call-update) | async-done | bytes 110608 | tf_op jit(solution)/shard_map/reduce_scatter | solution.py:370
  777.5 1.6 convert_bitcast_fusion.2
  783.2 40.1 %all-reduce.4 = (f32[128]{0:T(128)}, f32[128]{0:T(128)}, f32[128]{0:T(128)}, f32[768]{0:T(1024)S(1)}, f32[768]{0:T(1024)S(1)}) all-reduce(f32[128]{0:T(128)S(1)} %fusion.216, f32[128]{0:T(128)S(1)} %copy-done.92, f32[128]{0:T(128)S(1)} %copy-done.93, f32[768]{0:T(1024)S(1)} %copy-done.71, ...), channel_id=1, replica_groups=mesh['band'=8,'tok'=4] {'band','tok'}, use_global_device_ids=true, to_apply=%region_34.35 | all-reduce | flops 1920 | bytes 15360 | tf_op jit(solution)/shard_map/psum | solution.py:382
  824.4 64.5 %reduce-scatter.20.cloned.1.call-done = bf16[96,768]{1,0:T(8,128)(2,1)} async-done(((bf16[3072,768]{1,0:T(8,128)(2,1)}), bf16[96,768]{1,0:T(8,128)(2,1)}) %reduce-scatter.20.cloned.1.call-update) | async-done | bytes 147472 | tf_op jit(solution)/shard_map/reduce_scatter | solution.py:370
  888.9 1.6 convert_element_type.185
  890.6 110.7 %reduce-scatter.18.cloned.1.call-done = bf16[96,768]{1,0:T(8,128)(2,1)} async-done(((bf16[3072,768]{1,0:T(8,128)(2,1)}), bf16[96,768]{1,0:T(8,128)(2,1)}) %reduce-scatter.18.cloned.1.call-update) | async-done | bytes 147472 | tf_op jit(solution)/shard_map/reduce_scatter | solution.py:370
  1001.3 1.6 convert_bitcast_fusion.1
  1002.9 4.9 copy.187
  1007.8 6.8 copy.195
  1014.6 46.7 %reduce-scatter.10.cloned.1.call-done = bf16[6144,128]{1,0:T(8,128)(2,1)} async-done(((bf16[24576,128]{1,0:T(8,128)(2,1)}), bf16[6144,128]{1,0:T(8,128)(2,1)}) %reduce-scatter.10.cloned.1.call-update) | async-done | bytes 1572880 | tf_op jit(solution)/shard_map/reduce_scatter | solution.py:350
  1061.3 3.3 convert_element_type.180
  1064.6 145.3 %all-reduce.8.cloned.1.call-done = (f32[128,768]{1,0:T(8,128)}, f32[128,128]{1,0:T(8,128)}, f32[128,128]{1,0:T(8,128)}, f32[128,128]{1,0:T(8,128)}, f32[128,128]...) async-done(((f32[128,768]{1,0:T(8,128)}, f32[128,128]{1,0:T(8,128)}, f32[128,128]{1,0:T(8,128)}, f32[128,128]{1,0:T(8,128)}, f32[128,128]{1,0:T(8,128)}, ...) | async-done | bytes 2752528 | tf_op jit(solution)/shard_map/psum | solution.py:382
  1209.8 1.9 copy.237
  1211.7 1.5 copy.238
  1213.2 1.5 copy.239
  1214.6 1.5 copy.240
  1216.1 1.5 copy.241
  1217.6 2.3 copy.242
  (337 shorter events, 53.6 us)
Async XLA Ops:
  7.2 26.0 %copy-start = (f32[128,2048]{1,0:T(8,128)S(1)}, f32[128,2048]{1,0:T(8,128)}, u32[]{:S(2)}) copy-start(f32[128,2048]{1,0:T(8,128)} %param.34) | copy-start | bytes 3145732
  7.2 119.4 %all-gather.8.cloned.1.call-start = ((), (), s32[]{:S(2)}) async-start(), calls=%async_computation.9 | async-start | bytes 7864320 | tf_op jit(solution)/shard_map/all_gather | solution.py:272
  19.2 7.5 copy-start.90
  19.2 7.5 copy-start.94
  19.2 8.3 copy-start.60
  19.2 8.4 copy-start.40
  19.2 9.0 copy-start.38
  19.3 9.6 copy-start.36
  19.3 100.7 %all-to-all-start = ((bf16[8,8,32,4,256]{4,2,3,1,0:T(8,128)(2,1)}), bf16[8,8,32,4,256]{4,2,3,1,0:T(8,128)(2,1)}, u32[]{:S(2)}, u32[]{:S(2)}) async-start(bf16[8,8,32,4,256]{4,2,3,1,0:T(8,128)(2,1)} %copy.173), calls=%async_computation | async-start | bytes 8388608 | tf_op jit(solution)/shard_map/all_to_all | solution.py:268
  26.7 203.9 %reduce-scatter.8.cloned.1.call-start = ((), (), s32[]{:S(2)}) async-start(), calls=%async_computation.10 | async-start | bytes 3538944 | tf_op jit(solution)/shard_map/reduce_scatter | solution.py:302
  38.4 10.6 copy-start.82
  49.1 77.4 %copy-start.42 = (bf16[8,32,128]{2,1,0:T(8,128)(2,1)}, bf16[8,32,128]{2,1,0:T(8,128)(2,1)S(1)}, u32[]{:S(2)}) copy-start(bf16[8,32,128]{2,1,0:T(8,128)(2,1)S(1)} %fusion.153) | copy-start | bytes 196612
  135.7 11.2 copy-start.3
  157.0 105.0 %all-gather.10.cloned.1.call-start = ((), (), s32[]{:S(2)}) async-start(), calls=%async_computation.11 | async-start | bytes 4423680 | tf_op jit(solution)/shard_map/all_gather | solution.py:275
  157.8 123.2 %all-gather.12.cloned.1.call-start = ((), (), s32[]{:S(2)}) async-start(), calls=%async_computation.12 | async-start | bytes 1474560 | tf_op jit(solution)/shard_map/all_gather | solution.py:276
  158.3 161.5 %all-gather.14.cloned.1.call-start = ((), (), s32[]{:S(2)}) async-start(), calls=%async_computation.13 | async-start | bytes 5898240 | tf_op jit(solution)/shard_map/all_gather | solution.py:277
  158.9 199.9 %all-gather.16.cloned.1.call-start = ((), (), s32[]{:S(2)}) async-start(), calls=%async_computation.14 | async-start | bytes 5898240 | tf_op jit(solution)/shard_map/all_gather | solution.py:278
  159.5 282.0 %all-gather.18.cloned.1.call-start = ((), (), s32[]{:S(2)}) async-start(), calls=%async_computation.21 | async-start | bytes 3538944 | tf_op jit(solution)/shard_map/all_gather | solution.py:326
  162.8 216.3 %copy-start.87 = (pred[256]{0:T(512)(128)(4,1)}, pred[256]{0:T(512)(128)(4,1)S(1)}, u32[]{:S(2)}) copy-start(pred[256]{0:T(512)(128)(4,1)S(1)} %iota_compare_fusion.1) | copy-start | bytes 772
  162.8 99.3 %copy-start.58 = (f32[768]{0:T(1024)S(1)}, f32[768]{0:T(1024)}, u32[]{:S(2)}) copy-start(f32[768]{0:T(1024)} %param.42) | copy-start | bytes 9220
  165.0 97.1 %copy-start.41 = (f32[33,128]{1,0:T(8,128)}, f32[33,128]{1,0:T(8,128)S(1)}, u32[]{:S(2)}) copy-start(f32[33,128]{1,0:T(8,128)S(1)} %get-tuple-element.146) | copy-start | bytes 50692
  165.0 101.4 %copy-start.83 = (f32[33]{0:T(128)}, f32[33]{0:T(128)S(1)}, u32[]{:S(2)}) copy-start(f32[33]{0:T(128)S(1)} %broadcast_multiply_fusion.6) | copy-start | bytes 400
  165.2 65.4 %copy-start.97 = (f32[33]{0:T(128)}, f32[33]{0:T(128)S(1)}, u32[]{:S(2)}) copy-start(f32[33]{0:T(128)S(1)} %multiply_reduce_fusion.10) | copy-start | bytes 400
  165.2 101.1 %copy-start.89 = (f32[33]{0:T(128)}, f32[33]{0:T(128)S(1)}, u32[]{:S(2)}) copy-start(f32[33]{0:T(128)S(1)} %fusion.220) | copy-start | bytes 400
  165.3 101.1 %copy-start.62 = (f32[1,33,128]{2,1,0:T(8,128)}, f32[1,33,128]{2,1,0:T(8,128)S(1)}, u32[]{:S(2)}) copy-start(f32[1,33,128]{2,1,0:T(8,128)S(1)} %multiply_bitcast_fusion) | copy-start | bytes 50692
  165.7 213.3 %copy-start.55 = (f32[768]{0:T(1024)}, f32[768]{0:T(1024)S(1)}, u32[]{:S(2)}) copy-start(f32[768]{0:T(1024)S(1)} %convolution_reduce_fusion) | copy-start | bytes 9220
  231.8 147.3 %copy-start.63 = (f32[256]{0:T(256)}, f32[256]{0:T(256)S(1)}, u32[]{:S(2)}) copy-start(f32[256]{0:T(256)S(1)} %broadcast_multiply_fusion.5) | copy-start | bytes 3076
  233.0 146.0 %copy-start.69 = (f32[256]{0:T(256)}, f32[256]{0:T(256)S(1)}, u32[]{:S(2)}) copy-start(f32[256]{0:T(256)S(1)} %fusion.214) | copy-start | bytes 3076
  270.4 10.6 copy-start.4
  271.9 48.0 %copy-start.67 = (f32[768]{0:T(1024)S(1)}, f32[768]{0:T(1024)}, u32[]{:S(2)}) copy-start(f32[768]{0:T(1024)} %param.43) | copy-start | bytes 9220
  283.0 84.5 %copy-start.5 = (f32[256,768]{1,0:T(8,128)}, f32[256,768]{1,0:T(8,128)S(1)}, u32[]{:S(2)}) copy-start(f32[256,768]{1,0:T(8,128)S(1)} %get-tuple-element.150) | copy-start | bytes 2359300
  283.0 84.5 %copy-start.72 = (f32[256]{0:T(256)}, f32[256]{0:T(256)S(1)}, u32[]{:S(2)}) copy-start(f32[256]{0:T(256)S(1)} %broadcast_multiply_fusion.4) | copy-start | bytes 3076
  283.2 84.3 %copy-start.76 = (f32[256]{0:T(256)}, f32[256]{0:T(256)S(1)}, u32[]{:S(2)}) copy-start(f32[256]{0:T(256)S(1)} %fusion.215) | copy-start | bytes 3076
  380.9 166.2 %reduce-scatter.12.cloned.1.call-start = ((), (), s32[]{:S(2)}) async-start(), calls=%async_computation.16 | async-start | bytes 147456 | tf_op jit(solution)/shard_map/reduce_scatter | solution.py:346
  453.1 23.6 %slice-start = ((s8[6291456]{0:T(1024)(128)(4,1)}), s8[2097152]{0:T(1024)(128)(4,1)S(1)}, s32[]{:S(2)}) async-start(s8[6291456]{0:T(1024)(128)(4,1)} %bitcast.328), calls=%async_computation.23 | async-start | bytes 4194304
  481.2 189.0 %reduce-scatter.16.cloned.1.call-start = ((), (), s32[]{:S(2)}) async-start(), calls=%async_computation.18 | async-start | bytes 1216512 | tf_op jit(solution)/shard_map/reduce_scatter | solution.py:370
  484.1 293.4 %reduce-scatter.14.cloned.1.call-start = ((), (), s32[]{:S(2)}) async-start(), calls=%async_computation.17 | async-start | bytes 3649536 | tf_op jit(solution)/shard_map/reduce_scatter | solution.py:370
  487.2 401.7 %reduce-scatter.20.cloned.1.call-start = ((), (), s32[]{:S(2)}) async-start(), calls=%async_computation.20 | async-start | bytes 4866048 | tf_op jit(solution)/shard_map/reduce_scatter | solution.py:370
  492.4 508.9 %reduce-scatter.18.cloned.1.call-start = ((), (), s32[]{:S(2)}) async-start(), calls=%async_computation.19 | async-start | bytes 4866048 | tf_op jit(solution)/shard_map/reduce_scatter | solution.py:370
  497.7 563.6 %reduce-scatter.10.cloned.1.call-start = ((), (), s32[]{:S(2)}) async-start(), calls=%async_computation.15 | async-start | bytes 7864320 | tf_op jit(solution)/shard_map/reduce_scatter | solution.py:350
  536.0 14.4 %copy-start.13 = (f32[2048,128]{1,0:T(8,128)S(1)}, f32[2048,128]{1,0:T(8,128)}, u32[]{:S(2)}) copy-start(f32[2048,128]{1,0:T(8,128)} %param.35) | copy-start | bytes 3145732
  536.0 14.4 %copy-start.23 = (f32[33,2048]{1,0:T(8,128)S(1)}, f32[33,2048]{1,0:T(8,128)}, u32[]{:S(2)}) copy-start(f32[33,2048]{1,0:T(8,128)} %copy-done.22) | copy-start | bytes 811012
  536.0 14.4 %copy-start.26 = (f32[33,2048]{1,0:T(8,128)S(1)}, f32[33,2048]{1,0:T(8,128)}, u32[]{:S(2)}) copy-start(f32[33,2048]{1,0:T(8,128)} %copy-done.25) | copy-start | bytes 811012
  536.0 466.9 %all-to-all-start.1 = ((bf16[8,8,32,4,256]{4,2,3,1,0:T(8,128)(2,1)}), bf16[8,8,32,4,256]{4,2,3,1,0:T(8,128)(2,1)}, u32[]{:S(2)}, u32[]{:S(2)}) async-start(bf16[8,8,32,4,256]{4,2,3,1,0:T(8,128)(2,1)} %bitcast.333), calls=%async_computation.2 | async-start | bytes 8388608 | tf_op jit(solution)/shard_map/all_to_all | solution.py:333
  540.7 669.1 %all-reduce.8.cloned.1.call-start = ((), (), s32[]{:S(2)}) async-start(), calls=%async_computation.22 | async-start | bytes 5505024 | tf_op jit(solution)/shard_map/psum | solution.py:382
  547.2 7.4 copy-start.35
  547.2 7.6 copy-start.31
  547.2 7.6 copy-start.54
  547.2 7.6 copy-start.66
  547.2 7.6 copy-start.84
  547.2 8.0 copy-start.50
  547.2 8.0 copy-start.86
  547.2 8.2 copy-start.61
  547.2 9.1 copy-start.48
  547.3 11.5 copy-start.52
  550.5 11.2 copy-start.24
  550.5 11.2 copy-start.27
  564.5 214.6 %copy-start.37 = (f32[128,128]{1,0:T(8,128)S(1)}, f32[128,128]{1,0:T(8,128)}, u32[]{:S(2)}) copy-start(f32[128,128]{1,0:T(8,128)} %param.30) | copy-start | bytes 196612
  564.6 215.7 %copy-start.39 = (f32[128,128]{1,0:T(8,128)S(1)}, f32[128,128]{1,0:T(8,128)}, u32[]{:S(2)}) copy-start(f32[128,128]{1,0:T(8,128)} %param.31) | copy-start | bytes 196612
  564.6 218.6 %copy-start.71 = (f32[768]{0:T(1024)S(1)}, f32[768]{0:T(1024)}, u32[]{:S(2)}) copy-start(f32[768]{0:T(1024)} %get-tuple-element.100) | copy-start | bytes 9220
  564.6 218.6 %copy-start.91 = (f32[768]{0:T(1024)S(1)}, f32[768]{0:T(1024)}, u32[]{:S(2)}) copy-start(f32[768]{0:T(1024)} %get-tuple-element.98) | copy-start | bytes 9220
  564.6 218.6 %copy-start.92 = (f32[128]{0:T(128)S(1)}, f32[128]{0:T(128)}, u32[]{:S(2)}) copy-start(f32[128]{0:T(128)} %get-tuple-element.102) | copy-start | bytes 1540
  564.6 218.6 %copy-start.93 = (f32[128]{0:T(128)S(1)}, f32[128]{0:T(128)}, u32[]{:S(2)}) copy-start(f32[128]{0:T(128)} %get-tuple-element.104) | copy-start | bytes 1540
  1209.8 10.0 copy-start.29
  (54 other events, 162.0 us)
Sparse Core Ops, SparseCore 0:
  9.6 49.0 all-gather.7
  157.1 73.3 reduce-scatter.7
  232.2 29.8 all-gather.9
  263.5 17.4 all-gather.11
  282.4 37.4 all-gather.13
  321.3 37.4 all-gather.15
  381.0 60.4 all-gather.17
  481.4 59.5 reduce-scatter.11
  546.0 124.2 reduce-scatter.15
  675.5 101.9 reduce-scatter.13
  783.0 105.8 reduce-scatter.19
  895.2 106.0 reduce-scatter.17
  1003.8 57.4 reduce-scatter.9
  1069.9 139.9 all-reduce.7

commit v2 on v1

--- a/solution.py
+++ b/solution.py
@@ -1,8 +1,11 @@
+import functools
 import math
 
 import jax
 import jax.numpy as jnp
 from jax import lax
+from jax.experimental import pallas as pl
+from jax.experimental.pallas import tpu as pltpu
 from jax.sharding import PartitionSpec as P
 
 HD = 64
@@ -12,6 +15,1094 @@
 EPS_BLOCK = 1e-06
 EPS_HYPER = 1e-05
 PRECISE = lax.Precision.HIGHEST
+
+
+MESH = pl.DeviceIdType.MESH
+
+
+def mesh_bits():
+    tok_bits = (lax.axis_size("tok") - 1).bit_length()
+    band_bits = (lax.axis_size("band") - 1).bit_length()
+    dims = [("band", b) for b in reversed(range(band_bits))]
+    dims += [("tok", b) for b in reversed(range(tok_bits))]
+    return dims, band_bits, tok_bits
+
+
+def own_bit(axis, bit):
+    return lax.rem(lax.div(lax.axis_index(axis), 1 << bit), 2)
+
+
+def partner_of(axis, bit):
+    place = lax.axis_index(axis)
+    mine = own_bit(axis, bit)
+    other = place + (1 - 2 * mine) * (1 << bit)
+    band, tok = lax.axis_index("band"), lax.axis_index("tok")
+    return (other, tok) if axis == "band" else (band, other)
+
+
+def halving_order(which, band_bits, tok_bits):
+    tok = [("tok", b) for b in range(tok_bits)]
+    band = [("band", b) for b in range(band_bits)]
+    if which == 2:
+        return tok
+    if which == 0:
+        return tok + band
+    return tok[:1] + band[:1] + tok[1:] + band[1:]
+
+
+def pick(remaining, axis_bit, value):
+    place = remaining.index(axis_bit)
+    return tuple([slice(None)] * place + [value])
+
+
+def add_block(dest, left, right):
+    lead = dest.shape[:-2]
+
+    def one(index):
+        spot = []
+        for size in reversed(lead):
+            spot.insert(0, lax.rem(index, size))
+            index = lax.div(index, size)
+        spot = tuple(spot)
+        dest[spot] = (left(spot) + right(spot)).astype(dest.dtype)
+
+    pl.loop(0, math.prod(lead))(one)
+
+
+def wide_blocks(shapes, piece):
+    blocks, start = [], 0
+    for index, (rows, columns) in enumerate(shapes):
+        for part in range(columns // 128):
+            row = 0
+            while row < rows:
+                inside = start % piece
+                size = min(rows - row, piece - inside)
+                blocks.append((index, row, part, start // piece, inside, size))
+                row += size
+                start += size
+    return blocks, start
+
+
+def segment_spot(segment, count):
+    return tuple((segment >> (count - 1 - bit)) & 1 for bit in range(count))
+
+
+class Sums:
+    def __init__(
+        self, streams, sources, outputs, own, landing, send_sem, recv_sem, own_sem, buffer=None
+    ):
+        self.buffer = buffer
+        self.streams, self.sources, self.outputs = streams, sources, outputs
+        self.own, self.landing = own, landing
+        self.send_sem, self.recv_sem, self.own_sem = send_sem, recv_sem, own_sem
+        self.flying, self.local = {}, {}
+
+    def part(self, stream, value):
+        entry = self.streams[stream]
+        spot = pick(entry["span"], entry["order"][0], value)
+        spot = spot + (slice(None),) * (len(entry["span"]) - len(spot))
+        rows = pl.ds(entry["start"], entry["rows"])
+        return self.sources[entry["source"]].at[spot + (rows,)]
+
+    def fetch(self, stream):
+        entry = self.streams[stream]
+        if entry["fetch"]:
+            slot = stream % len(self.own)
+            whole = (slice(None),) * (len(entry["span"]) - 1)
+            target = self.own[slot].at[whole + (pl.ds(0, entry["rows"]),)]
+            copy = pltpu.make_async_copy(
+                self.part(stream, own_bit(*entry["order"][0])), target, self.own_sem.at[slot]
+            )
+            copy.start()
+            self.local[stream] = (copy, target)
+
+    def send(self, stream, stage, source):
+        axis, bit = self.streams[stream]["order"][stage]
+        copy = pltpu.make_async_remote_copy(
+            src_ref=source,
+            dst_ref=self.landing[stream][stage],
+            send_sem=self.send_sem.at[stream, stage],
+            recv_sem=self.recv_sem.at[stream, stage],
+            device_id=partner_of(axis, bit),
+            device_id_type=MESH,
+        )
+        copy.start()
+        self.flying[stream, stage] = copy
+
+    def begin(self, stream):
+        first = self.streams[stream]["order"][0]
+        self.send(stream, 0, self.part(stream, 1 - own_bit(*first)))
+
+    def advance(self, stream, stage):
+        entry = self.streams[stream]
+        order, span = entry["order"], entry["span"]
+        if stage >= len(order):
+            return
+        remaining = [d for d in span if d not in order[:stage]]
+        axis_bit = order[stage]
+        after = [d for d in remaining if d != axis_bit]
+        self.flying[stream, stage].wait_recv()
+        land = self.landing[stream][stage]
+        if stage > 0:
+            held = self.landing[stream][stage - 1].at[
+                pick(remaining, axis_bit, own_bit(*axis_bit))
+            ]
+        elif stream in self.local:
+            self.local[stream][0].wait()
+            held = self.local[stream][1]
+        else:
+            held = self.part(stream, own_bit(*axis_bit))
+        if stage == len(order) - 1 and entry["out"] is not None:
+            total = land[...].astype(jnp.float32) + held[...].astype(jnp.float32)
+            rows = pl.ds(entry["start"], entry["rows"])
+            if entry["fetch"]:
+                self.outputs[entry["out"]][rows] = total * entry["scale"]
+            else:
+                buffer, sem = self.buffer
+                buffer[...] = total * entry["scale"]
+                copy = pltpu.make_async_copy(buffer, self.outputs[entry["out"]].at[rows], sem)
+                copy.start()
+                copy.wait()
+        else:
+            add_block(
+                land,
+                lambda spot: land[spot].astype(jnp.float32),
+                lambda spot: held[spot].astype(jnp.float32),
+            )
+            if stage < len(order) - 1:
+                following = order[stage + 1]
+                self.send(
+                    stream, stage + 1, land.at[pick(after, following, 1 - own_bit(*following))]
+                )
+
+    def drain(self):
+        for copy in self.flying.values():
+            copy.wait_send()
+
+
+class Spread:
+    def __init__(self, dims, order, whole, send_sem, recv_sem):
+        self.dims, self.order, self.whole = dims, list(reversed(order)), whole
+        self.send_sem, self.recv_sem = send_sem, recv_sem
+        self.spot = [own_bit(*d) if d in order else slice(None) for d in dims]
+        self.copies = []
+
+    def start(self):
+        step = len(self.copies)
+        view = self.whole.at[tuple(self.spot)]
+        copy = pltpu.make_async_remote_copy(
+            src_ref=view,
+            dst_ref=view,
+            send_sem=self.send_sem.at[step],
+            recv_sem=self.recv_sem.at[step],
+            device_id=partner_of(*self.order[step]),
+            device_id_type=MESH,
+        )
+        copy.start()
+        self.copies.append(copy)
+
+    def finish(self):
+        self.copies[-1].wait()
+        self.spot[self.dims.index(self.order[len(self.copies) - 1])] = slice(None)
+
+
+def pack_blocks(blocks, used, packed, wide, stages):
+    for index, row, part, segment, inside, size in blocks:
+        packed[segment_spot(segment, stages) + (pl.ds(inside, size),)] = wide[index](
+            pl.ds(row, size), pl.ds(part * 128, 128)
+        ).astype(packed.dtype)
+    piece = packed.shape[-2]
+    while used < piece << stages:
+        size = piece - used % piece
+        packed[segment_spot(used // piece, stages) + (pl.ds(used % piece, size),)] = jnp.zeros(
+            (size, 128), packed.dtype
+        )
+        used += size
+
+
+def unpack_blocks(blocks, whole, wide_out, stages):
+    for index, row, part, segment, inside, size in blocks:
+        wide_out[index][pl.ds(row, size), pl.ds(part * 128, 128)] = whole[
+            segment_spot(segment, stages) + (pl.ds(inside, size),)
+        ].astype(jnp.float32)
+
+
+def reduce_kernel(plan, blocks, used, *refs):
+    streams, dims = plan["streams"], plan["dims"]
+    count, stages = len(streams), len(dims)
+    pos = plan["bulk"]
+    inputs = list(refs[:pos])
+    wide = refs[pos : pos + plan["wide"]]
+    pos += plan["wide"]
+    outputs = refs[pos : pos + plan["bulk"]]
+    pos += plan["bulk"]
+    wide_out = refs[pos : pos + plan["wide"]]
+    pos += plan["wide"]
+    own = refs[pos : pos + count - 1]
+    pos += count - 1
+    landing = []
+    for stream in streams:
+        landing.append(refs[pos : pos + len(stream["order"])])
+        pos += len(stream["order"])
+    packed, whole, send_sem, recv_sem, own_sem, gather_send, gather_recv = refs[pos:]
+    barrier = pltpu.get_barrier_semaphore()
+    for axis, bit in dims:
+        pl.semaphore_signal(barrier, inc=1, device_id=partner_of(axis, bit), device_id_type=MESH)
+    pl.semaphore_wait(barrier, stages)
+    sums = Sums(
+        streams, inputs + [packed], outputs, own, landing, send_sem, recv_sem, own_sem
+    )
+    for stream in range(count - 1):
+        sums.begin(stream)
+        sums.fetch(stream)
+    pack_blocks(
+        blocks, used, packed, [lambda r, c, ref=ref: ref[r, c] for ref in wide], stages
+    )
+    sums.begin(count - 1)
+    for stage in range(stages):
+        for stream in range(count):
+            sums.advance(stream, stage)
+    spread = Spread(dims, streams[-1]["order"], whole, gather_send, gather_recv)
+    whole[tuple(spread.spot)] = landing[count - 1][stages - 1][...]
+    for _ in range(stages):
+        spread.start()
+        spread.finish()
+    unpack_blocks(blocks, whole, wide_out, stages)
+    sums.drain()
+
+
+def stream_entry(source, out, start, rows, order, dims, fetch, scale=1.0):
+    return {
+        "source": source,
+        "out": out,
+        "start": start,
+        "rows": rows,
+        "order": order,
+        "span": [d for d in dims if d in order],
+        "fetch": fetch,
+        "scale": scale,
+    }
+
+
+def landing_shapes(entry, lanes):
+    stages = len(entry["order"])
+    return [
+        pltpu.VMEM((2,) * (stages - 1 - stage) + (entry["rows"], lanes), jnp.bfloat16)
+        for stage in range(stages)
+    ]
+
+
+def wide_plan(shapes, devices):
+    used = sum(math.prod(shape) for shape in shapes) // 128
+    piece = -(-used // (16 * devices)) * 16
+    return wide_blocks(shapes, piece)[0], used, piece
+
+
+def row_chunks(rows, chunks):
+    size = -(-rows // chunks // 8) * 8
+    return [(start, min(size, rows - start)) for start in range(0, rows, size)]
+
+
+def reduce_all(arrays, whiches, chunks, wide, collective_id):
+    dims, band_bits, tok_bits = mesh_bits()
+    low, everything = jnp.bfloat16, len(dims)
+    split, outs, own, landing, streams = [], [], [], [], []
+    for k, array in enumerate(arrays):
+        order = halving_order(whiches[k], band_bits, tok_bits)
+        stages = len(order)
+        rows, lanes = array.shape[0] >> stages, array.shape[1]
+        split.append(array.reshape((2,) * stages + (rows, lanes)))
+        outs.append(jax.ShapeDtypeStruct((rows, lanes), jnp.float32))
+        for start, size in row_chunks(rows, chunks[k]):
+            streams.append(stream_entry(k, k, start, size, order, dims, True))
+            own.append(pltpu.VMEM((2,) * (stages - 1) + (size, lanes), low))
+            landing += landing_shapes(streams[-1], lanes)
+    blocks, used, piece = wide_plan([part.shape for part in wide], 1 << everything)
+    order = halving_order(0, band_bits, tok_bits)
+    streams.append(stream_entry(len(arrays), None, 0, piece, order, dims, False))
+    landing += landing_shapes(streams[-1], 128)
+    outs += [jax.ShapeDtypeStruct(part.shape, jnp.float32) for part in wide]
+    count = len(streams)
+    plan = {"streams": streams, "dims": dims, "bulk": len(arrays), "wide": len(wide)}
+    sent = sum(a.size for a in arrays)
+    space = (2,) * everything + (piece, 128)
+    return pl.pallas_call(
+        functools.partial(reduce_kernel, plan, blocks, used),
+        out_shape=outs,
+        in_specs=[pl.BlockSpec(memory_space=pl.ANY)] * len(arrays)
+        + [pl.BlockSpec(memory_space=pltpu.VMEM)] * len(wide),
+        out_specs=[pl.BlockSpec(memory_space=pltpu.VMEM)] * len(outs),
+        scratch_shapes=own
+        + landing
+        + [
+            pltpu.VMEM(space, low),
+            pltpu.VMEM(space, low),
+            pltpu.SemaphoreType.DMA((count, everything)),
+            pltpu.SemaphoreType.DMA((count, everything)),
+            pltpu.SemaphoreType.DMA((count,)),
+            pltpu.SemaphoreType.DMA((everything,)),
+            pltpu.SemaphoreType.DMA((everything,)),
+        ],
+        compiler_params=pltpu.CompilerParams(
+            collective_id=collective_id, has_side_effects=True, vmem_limit_bytes=60 << 20
+        ),
+        cost_estimate=pl.CostEstimate(flops=2 * sent, bytes_accessed=40 * sent, transcendentals=0),
+    )(*split, *wide)
+
+
+def turn_kernel(in_ref, out_ref, lines):
+    bands = in_ref.shape[1]
+    halves, rows = lines.shape[:2]
+    for band in range(bands):
+        turned = in_ref[0, band].astype(jnp.float32).T
+        for half in range(halves):
+            lines[half, pl.ds(band, rows // bands, stride=bands), :] = turned[
+                :, half * 128 : (half + 1) * 128
+            ]
+    for half in range(halves):
+        out_ref[:, 0, :, pl.ds(half * 128, 128)] = (
+            lines[half].astype(out_ref.dtype).reshape(*out_ref.shape[:1], -1, 128)
+        )
+
+
+def turn_pixels(pixels, owners):
+    images, bands, slot, pixel_count = pixels.shape
+    share = pixel_count // owners * bands
+    return pl.pallas_call(
+        turn_kernel,
+        grid=(images,),
+        out_shape=jax.ShapeDtypeStruct((owners, images, share, slot), pixels.dtype),
+        in_specs=[pl.BlockSpec((1, bands, slot, pixel_count), lambda i: (i, 0, 0, 0))],
+        out_specs=pl.BlockSpec((owners, 1, share, slot), lambda i: (0, i, 0, 0)),
+        scratch_shapes=[pltpu.VMEM((slot // 128, pixel_count * bands, 128), jnp.float32)],
+        compiler_params=pltpu.CompilerParams(vmem_limit_bytes=20 << 20),
+    )(pixels)
+
+
+def unturn_kernel(in_ref, out_ref, lines):
+    bands = out_ref.shape[1]
+    halves, rows = lines.shape[:2]
+    for half in range(halves):
+        lines[half] = (
+            in_ref[:, 0, :, pl.ds(half * 128, 128)].astype(jnp.float32).reshape(rows, 128)
+        )
+    for band in range(bands):
+        for half in range(halves):
+            piece = lines[half, pl.ds(band, rows // bands, stride=bands), :]
+            out_ref[0, band, pl.ds(half * 128, 128), :] = piece.T.astype(out_ref.dtype)
+
+
+def unturn_pixels(blocks, shape):
+    owners, images, share, slot = blocks.shape
+    bands, pixel_count = shape[1], shape[3]
+    return pl.pallas_call(
+        unturn_kernel,
+        grid=(images,),
+        out_shape=jax.ShapeDtypeStruct(shape, blocks.dtype),
+        in_specs=[pl.BlockSpec((owners, 1, share, slot), lambda i: (0, i, 0, 0))],
+        out_specs=pl.BlockSpec((1, bands, slot, pixel_count), lambda i: (i, 0, 0, 0)),
+        scratch_shapes=[pltpu.VMEM((slot // 128, pixel_count * bands, 128), jnp.float32)],
+        compiler_params=pltpu.CompilerParams(vmem_limit_bytes=20 << 20),
+    )(blocks)
+
+
+def at_band(place):
+    return (place, lax.axis_index("tok"))
+
+
+def pair_place():
+    band = lax.axis_index("band")
+    return lax.div(band, 2), lax.rem(band, 2)
+
+
+def first_half(shape):
+    return lax.rem(lax.broadcasted_iota(jnp.int32, shape, len(shape) - 2), 8) < 4
+
+
+def make_kernels(gen_ref, even_ref, odd_ref, kern_ref, factor):
+    pixel_share, model_dim = gen_ref.shape[:2]
+    pairs, _, owners, _, _ = kern_ref.shape
+    width = 256
+
+    @pl.loop(0, pixel_share // 4)
+    def _(quad):
+        @pl.loop(0, model_dim // width)
+        def _(part):
+            columns = pl.ds(pl.multiple_of(part * width, width), width)
+            pieces = []
+            for offset in range(4):
+                rows = (even_ref, odd_ref)[offset % 2][...]
+                piece = lax.dot_general(
+                    rows,
+                    gen_ref[quad * 4 + offset, columns, :],
+                    (((1,), (1,)), ((), ())),
+                    preferred_element_type=jnp.float32,
+                )
+                pieces.append((piece * factor).reshape(pairs * owners, 8, width))
+            top = first_half(pieces[0].shape)
+            even, odd = [], []
+            for a, b in ((pieces[0], pieces[1]), (pieces[2], pieces[3])):
+                even.append(jnp.where(top, a, b))
+                odd.append(pltpu.roll(jnp.where(top, b, a), 4, 1))
+            rows = pl.ds(pl.multiple_of(quad * 16, 16), 16)
+            for parity, both in ((0, even), (1, odd)):
+                block = jnp.concatenate(both, axis=1).astype(jnp.bfloat16)
+                kern_ref[:, parity, :, rows, columns] = block.reshape(pairs, owners, 16, width)
+
+
+def embed_kernel(
+    factor,
+    gen_hbm,
+    pix_hbm,
+    even_ref,
+    odd_ref,
+    out_ref,
+    gen_ref,
+    pix_ref,
+    kern_ref,
+    y_out,
+    y_in,
+    z_out,
+    z_in,
+    kept,
+    load_sem,
+    y_send,
+    y_recv,
+    z_send,
+    z_recv,
+):
+    pairs = kern_ref.shape[0]
+    depth, side = pairs, lax.rem(lax.axis_index("band"), 2)
+    place = lax.div(lax.axis_index("band"), 2)
+    loads = [
+        pltpu.make_async_copy(gen_hbm, gen_ref, load_sem.at[0]),
+        pltpu.make_async_copy(pix_hbm, pix_ref, load_sem.at[1]),
+    ]
+    for load in loads:
+        load.start()
+    barrier = pltpu.get_barrier_semaphore()
+    pl.semaphore_signal(
+        barrier, inc=1, device_id=at_band(place * 2 + 1 - side), device_id_type=MESH
+    )
+    for step in range(depth - 1):
+        target = lax.rem(place + 1 + step, depth)
+        pl.semaphore_signal(
+            barrier, inc=1, device_id=at_band(target * 2 + side), device_id_type=MESH
+        )
+    loads[0].wait()
+    make_kernels(gen_ref, even_ref, odd_ref, kern_ref, factor)
+    loads[1].wait()
+    pl.semaphore_wait(barrier, depth)
+    width = 256
+
+    def conv(pair, parity, store):
+        slot, inner = kern_ref.shape[3], pix_ref.shape[3]
+        owners = kern_ref.shape[2]
+        left = pix_ref[:, pair * 2 + parity].reshape(owners * slot, inner).T
+
+        @pl.loop(0, kern_ref.shape[4] // width)
+        def _(part):
+            columns = pl.ds(pl.multiple_of(part * width, width), width)
+            right = kern_ref[pair, parity, :, :, columns].reshape(owners * slot, width)
+            store(
+                columns,
+                jnp.dot(left, right, preferred_element_type=jnp.float32),
+            )
+
+    def y_copy(step):
+        return pltpu.make_async_remote_copy(
+            src_ref=y_out.at[step],
+            dst_ref=y_in.at[step],
+            send_sem=y_send.at[step],
+            recv_sem=y_recv.at[step],
+            device_id=at_band(place * 2 + 1 - side),
+            device_id_type=MESH,
+        )
+
+    def z_copy(step):
+        return pltpu.make_async_remote_copy(
+            src_ref=z_out.at[step],
+            dst_ref=z_in.at[step],
+            send_sem=z_send.at[step],
+            recv_sem=z_recv.at[step],
+            device_id=at_band(lax.rem(place + 1 + step, depth) * 2 + side),
+            device_id_type=MESH,
+        )
+
+    @pl.loop(0, depth)
+    def _(step):
+        def store(columns, value):
+            y_out[step, :, columns] = value.astype(y_out.dtype)
+
+        conv(lax.rem(place + 1 + step, depth), 1 - side, store)
+        y_copy(step).start()
+
+    @pl.loop(0, depth)
+    def _(step):
+        def store(columns, value):
+            kept[:, columns] = value
+
+        conv(lax.rem(place + 1 + step, depth), side, store)
+        y_copy(step).wait_recv()
+        total = kept[...] + y_in[step].astype(jnp.float32)
+
+        @pl.when(step < depth - 1)
+        def _():
+            z_out[step] = total.astype(z_out.dtype)
+            z_copy(step).start()
+
+        @pl.when(step == depth - 1)
+        def _():
+            out_ref[...] = total
+
+    @pl.loop(0, depth - 1)
+    def _(step):
+        z_copy(step).wait_recv()
+        out_ref[...] += z_in[step].astype(jnp.float32)
+
+    @pl.loop(0, depth)
+    def _(step):
+        y_copy(step).wait_send()
+
+    @pl.loop(0, depth - 1)
+    def _(step):
+        z_copy(step).wait_send()
+
+
+def embed_parts(gen_grid, pix, even, odd, model_dim, factor, collective_id):
+    owners, images, share, slot = pix.shape
+    depth = owners // 2
+    low = jnp.bfloat16
+    return pl.pallas_call(
+        functools.partial(embed_kernel, factor),
+        out_shape=jax.ShapeDtypeStruct((slot, model_dim), jnp.float32),
+        in_specs=[pl.BlockSpec(memory_space=pl.ANY)] * 2
+        + [pl.BlockSpec(memory_space=pltpu.VMEM)] * 2,
+        out_specs=pl.BlockSpec(memory_space=pltpu.VMEM),
+        scratch_shapes=[
+            pltpu.VMEM(gen_grid.shape, low),
+            pltpu.VMEM(pix.shape, low),
+            pltpu.VMEM((images // 2, 2, owners, share, model_dim), low),
+            pltpu.VMEM((depth, slot, model_dim), low),
+            pltpu.VMEM((depth, slot, model_dim), low),
+            pltpu.VMEM((depth - 1, slot, model_dim), low),
+            pltpu.VMEM((depth - 1, slot, model_dim), low),
+            pltpu.VMEM((slot, model_dim), jnp.float32),
+            pltpu.SemaphoreType.DMA((2,)),
+            pltpu.SemaphoreType.DMA((depth,)),
+            pltpu.SemaphoreType.DMA((depth,)),
+            pltpu.SemaphoreType.DMA((depth - 1,)),
+            pltpu.SemaphoreType.DMA((depth - 1,)),
+        ],
+        compiler_params=pltpu.CompilerParams(
+            collective_id=collective_id, has_side_effects=True, vmem_limit_bytes=60 << 20
+        ),
+        cost_estimate=pl.CostEstimate(
+            flops=10**10, bytes_accessed=12 * 10**7, transcendentals=0
+        ),
+    )(gen_grid, pix, even, odd)
+
+
+def tail_kernel(factor, plan, *refs):
+    streams, dims, blocks, used = plan["streams"], plan["dims"], plan["blocks"], plan["used"]
+    count, stages = len(streams), len(dims)
+    bulk = plan["bulk"]
+    refs = list(refs)
+
+    def take(number):
+        taken = refs[:number]
+        del refs[:number]
+        return taken
+
+    gen_hbm, pix_hbm = take(2)
+    weights_in = take(bulk)
+    low_ref, even_ref, odd_ref, feature_ref, token_ref, bias_grad_ref = take(6)
+    params = take(8)
+    gen_b_grad, gain_lines = take(2)
+    (pixel_land,) = take(1)
+    outputs = take(bulk + 1)
+    wide_out = take(8)
+    gen_ref, pix_ref, kern_ref, gath, stage_ref, part_ref, part_in, wide_ref = take(8)
+    expand_ref, shrink_ref = wide_out[4:6]
+    own = take(2)
+    landing = [take(len(stream["order"])) for stream in streams]
+    packed, whole = take(2)
+    load_sem, near_send, far_send, relay_send, block_recv, part_send, part_recv = take(7)
+    send_sem, recv_sem, own_sem, gather_send, gather_recv = take(5)
+    pixel_send, pixel_recv, pixel_own = take(3)
+    sum_in, sum_send, sum_recv, share_send, share_recv, out_buffer, out_sem = take(7)
+
+    depth = kern_ref.shape[0]
+    owners, share = kern_ref.shape[2], kern_ref.shape[3]
+    slot, model_dim = low_ref.shape
+    place, side = pair_place()
+    mine = place * 2 + side
+    beside = place * 2 + 1 - side
+    dk_ref = kern_ref.reshape(depth, gen_ref.shape[0] // 2, 2, owners * 8, model_dim)
+    tok_dims = [d for d in dims if d[0] == "tok"]
+    loads = [
+        pltpu.make_async_copy(gen_hbm, gen_ref, load_sem.at[0]),
+        pltpu.make_async_copy(pix_hbm, pix_ref, load_sem.at[1]),
+        pltpu.make_async_copy(params[4], expand_ref, load_sem.at[2]),
+        pltpu.make_async_copy(params[5], shrink_ref, load_sem.at[3]),
+    ]
+    for load in loads:
+        load.start()
+    barrier = pltpu.get_barrier_semaphore()
+    for step in range(1, owners):
+        pl.semaphore_signal(
+            barrier,
+            inc=1,
+            device_id=at_band(lax.rem(mine + step, owners)),
+            device_id_type=MESH,
+        )
+    for axis, bit in tok_dims:
+        pl.semaphore_signal(barrier, inc=1, device_id=partner_of(axis, bit), device_id_type=MESH)
+    pl.semaphore_wait(barrier, owners - 1 + len(tok_dims))
+
+    def block_copy(source, block, target, sem):
+        return pltpu.make_async_remote_copy(
+            src_ref=source,
+            dst_ref=gath.at[block],
+            send_sem=sem,
+            recv_sem=block_recv.at[block],
+            device_id=at_band(target),
+            device_id_type=MESH,
+        )
+
+    near = block_copy(low_ref, mine, beside, near_send)
+    far = [
+        block_copy(
+            low_ref, mine, lax.rem(place + step, depth) * 2 + side, far_send.at[step - 1]
+        )
+        for step in range(1, depth)
+    ]
+    for copy in far[:1] + [near] + far[1:]:
+        copy.start()
+    bits = (2,) * len(tok_dims)
+    segments = gen_ref.reshape(bits + (gen_ref.shape[0] * model_dim >> len(bits), gen_ref.shape[2]))
+    sums = Sums(
+        streams,
+        weights_in + [segments, packed],
+        outputs,
+        own,
+        landing,
+        send_sem,
+        recv_sem,
+        own_sem,
+        (out_buffer, out_sem),
+    )
+    heavy = [s for s in range(count) if streams[s]["source"] < bulk]
+    slices = [s for s in range(count) if streams[s]["source"] == bulk]
+    light = count - 1
+    for stream in heavy:
+        sums.begin(stream)
+    for stream in heavy[:2]:
+        sums.fetch(stream)
+    gath[mine] = low_ref[...]
+    loads[0].wait()
+    make_kernels(gen_ref, even_ref, odd_ref, kern_ref, factor)
+    for stream in heavy:
+        sums.advance(stream, 0)
+        if stream + 2 < len(heavy):
+            sums.fetch(stream + 2)
+    loads[1].wait()
+    width = 256
+
+    def relay(step):
+        block = lax.rem(place + step, depth) * 2 + side
+        return block_copy(gath.at[block], block, beside, relay_send.at[step - 1])
+
+    def pixel_copy(image, step):
+        target = lax.rem(mine + step, owners)
+        return pltpu.make_async_remote_copy(
+            src_ref=pix_ref.at[target, image],
+            dst_ref=pixel_land.at[mine, image],
+            send_sem=pixel_send.at[image, step - 1],
+            recv_sem=pixel_recv.at[image, step - 1],
+            device_id=at_band(target),
+            device_id_type=MESH,
+        )
+
+    def pixel_local(image):
+        return pltpu.make_async_copy(
+            pix_ref.at[mine, image], pixel_land.at[mine, image], pixel_own.at[image]
+        )
+
+    def pair_work(pair):
+        for parity in range(2):
+            image = pair * 2 + parity
+            rows = kern_ref[pair, parity].reshape(owners * share, model_dim)
+            turned = lax.dot_general(
+                rows, gath[image], (((1,), (1,)), ((), ())), preferred_element_type=jnp.float32
+            )
+            stage_ref[parity] = turned.astype(stage_ref.dtype).reshape(owners, share, slot)
+
+        @pl.loop(0, model_dim // width)
+        def _(part):
+            columns = pl.ds(pl.multiple_of(part * width, width), width)
+            both = []
+            for parity in range(2):
+                left = pix_ref[:, pair * 2 + parity].reshape(owners * share, slot)
+                both.append(
+                    jnp.dot(
+                        left,
+                        gath[pair * 2 + parity, :, columns],
+                        preferred_element_type=jnp.float32,
+                    ).reshape(owners * share // 8, 8, width)
+                )
+            even, odd = both[0], pltpu.roll(both[1], 4, 1)
+            top = first_half(even.shape)
+            for parity, value in (
+                (0, jnp.where(top, even, odd)),
+                (1, jnp.where(top, odd, even)),
+            ):
+                value = value.reshape(owners, share // 8, 8, width).transpose(1, 0, 2, 3)
+                value = value.reshape(share // 8, owners * 8, width)
+                dk_ref[pair, :, parity, :, columns] = value.astype(dk_ref.dtype)
+
+        for parity in range(2):
+            image = pair * 2 + parity
+            pix_ref[:, image] = stage_ref[parity]
+            pixel_local(image).start()
+
+    def pixel_send_pair(pair):
+        for parity in range(2):
+
+            @pl.loop(1, owners)
+            def _(step):
+                pixel_copy(pair * 2 + parity, step).start()
+
+    @pl.loop(0, depth)
+    def _(step):
+        pair = lax.rem(place + depth - step, depth)
+
+        @pl.when(step > 0)
+        def _():
+            block_copy(low_ref, pair * 2 + side, beside, near_send).wait_recv()
+            relay(depth - step).start()
+
+        block_copy(low_ref, pair * 2 + 1 - side, beside, near_send).wait_recv()
+        pair_work(pair)
+
+    def pair_at(step):
+        return lax.rem(place + depth - step, depth)
+
+    waiting = [pair_at(step) for step in range(depth)]
+    pixel_send_pair(waiting.pop(0))
+    part_ref[...] = jnp.zeros_like(part_ref)
+
+    @pl.loop(0, dk_ref.shape[1])
+    def _(duo):
+        for parity in range(2):
+            rows = dk_ref[:, duo, parity].reshape(depth * owners * 8, model_dim)
+            part_ref[parity] += jnp.dot(
+                rows, gen_ref[duo * 2 + parity], preferred_element_type=jnp.float32
+            ).reshape(depth, owners * 8, -1)
+            weight = lax.dot_general(
+                rows,
+                (even_ref, odd_ref)[parity][...],
+                (((0,), (0,)), ((), ())),
+                preferred_element_type=jnp.float32,
+            )
+            gen_ref[duo * 2 + parity] = weight.astype(gen_ref.dtype)
+
+    part_ref[...] = part_ref[...] * factor
+
+    def part_copy(step):
+        target = lax.rem(mine + step, owners)
+        return pltpu.make_async_remote_copy(
+            src_ref=part_ref.at[:, lax.div(target, 2)],
+            dst_ref=part_in.at[step - 1],
+            send_sem=part_send.at[step - 1],
+            recv_sem=part_recv.at[step - 1],
+            device_id=at_band(target),
+            device_id_type=MESH,
+        )
+
+    copies = [part_copy(step) for step in range(1, owners)]
+    for copy in copies:
+        copy.start()
+    for stream in slices:
+        sums.begin(stream)
+    early = len(heavy) // 2
+    for stream in heavy[:early]:
+        sums.advance(stream, 1)
+    total = part_ref[:, place]
+    for step, copy in enumerate(copies):
+        copy.wait_recv()
+        total += part_in[step]
+    pixel_send_pair(waiting.pop(0))
+    rows = total.shape[1]
+    bands = rows // 2
+    even_part = total[0].reshape(owners, 8, -1)
+    odd_part = total[1].reshape(owners, 8, -1)
+    low_rows = even_part + pltpu.roll(odd_part, 4, 1)
+    low_rows = jnp.where(side == 0, low_rows, pltpu.roll(low_rows, 4, 1))
+    low_rows = low_rows.reshape(rows, -1)
+    chooser = (
+        lax.broadcasted_iota(jnp.int32, (bands, rows), 1)
+        == lax.div(lax.broadcasted_iota(jnp.int32, (bands, rows), 0), 4) * 8
+        + lax.rem(lax.broadcasted_iota(jnp.int32, (bands, rows), 0), 4)
+    ).astype(jnp.float32)
+    d_band = precise_dot(chooser, low_rows)
+    hyper_dim = d_band.shape[1]
+    first_row = lax.broadcasted_iota(jnp.int32, (8, hyper_dim), 0) == 0
+    tokens = jnp.concatenate(
+        [feature_ref[...], jnp.where(first_row, token_ref[...], 0.0)], axis=0
+    )
+    cotangent = jnp.concatenate(
+        [d_band, jnp.where(first_row, bias_grad_ref[...], 0.0)], axis=0
+    )
+    width = 512
+    attention = tuple(params[place][...] for place in (0, 1, 2, 3, 6))
+    segment, segment_back = jax.vjp(
+        lambda t, p: hyper_attention(t, p, 1), tokens, attention
+    )
+    loads[2].wait()
+    loads[3].wait()
+    hyper_wide(segment, expand_ref, shrink_ref, wide_ref, width)
+    norm_back = jax.vjp(
+        lambda v, g: layer_norm(v, g, EPS_HYPER), wide_ref[...], params[7][...]
+    )[1]
+    d_total, second_grad = norm_back(cotangent)
+    hyper_wide_back(segment, d_total, expand_ref, shrink_ref, wide_ref, width)
+    token_grad, param_grads = segment_back(wide_ref[...])
+    small = [param_grads[0], param_grads[1], param_grads[2], param_grads[3]]
+    line_row = lax.broadcasted_iota(jnp.int32, gain_lines.shape, 0)
+    lines = gain_lines[...]
+    for row, value in enumerate((token_grad[bands : bands + 1], param_grads[4], second_grad)):
+        lines = jnp.where(line_row == row, value, lines)
+
+    def of_value(value):
+        return lambda r, c: value[
+            r.start : r.start + r.size, c.start : c.start + c.size
+        ]
+
+    def of_ref(ref):
+        return lambda r, c: ref[r, c]
+
+    wide = [of_value(value) for value in small]
+    wide += [of_ref(expand_ref), of_ref(shrink_ref), of_ref(gen_b_grad), of_value(lines)]
+    pack_blocks(blocks, used, packed, wide, stages)
+    sums.begin(light)
+    sums.advance(light, 0)
+    for stream in slices:
+        sums.advance(stream, 0)
+    for stream in heavy[early:]:
+        sums.advance(stream, 1)
+    while len(waiting) > 1:
+        pixel_send_pair(waiting.pop(0))
+    sums.advance(light, len(tok_dims) - 1)
+    piece = packed.shape[-2]
+    quarter = landing[light][-1].reshape(owners, piece, 128)
+
+    def sum_copy(step):
+        target = lax.rem(mine + step, owners)
+        return pltpu.make_async_remote_copy(
+            src_ref=quarter.at[target],
+            dst_ref=sum_in.at[step - 1],
+            send_sem=sum_send.at[step - 1],
+            recv_sem=sum_recv.at[step - 1],
+            device_id=at_band(target),
+            device_id_type=MESH,
+        )
+
+    own_tok = tuple(own_bit(*d) for d in tok_dims)
+    spread_view = whole.reshape((owners,) + bits + (piece, 128))
+
+    def share_copy(block, target, step):
+        return pltpu.make_async_remote_copy(
+            src_ref=spread_view.at[(block,) + own_tok],
+            dst_ref=spread_view.at[(block,) + own_tok],
+            send_sem=share_send.at[step - 1],
+            recv_sem=share_recv.at[step - 1],
+            device_id=at_band(target),
+            device_id_type=MESH,
+        )
+
+    moves = [sum_copy(step) for step in range(1, owners)]
+    for copy in moves:
+        copy.start()
+    pixel_send_pair(waiting.pop(0))
+    for stream in heavy:
+        sums.advance(stream, 2)
+    light_total = quarter[mine].astype(jnp.float32)
+    for step, copy in enumerate(moves):
+        copy.wait_recv()
+        light_total += sum_in[step].astype(jnp.float32)
+    spread_view[(mine,) + own_tok] = light_total.astype(whole.dtype)
+    shares = [
+        share_copy(mine, lax.rem(mine + step, owners), step) for step in range(1, owners)
+    ]
+    for copy in shares:
+        copy.start()
+    for stage in range(3, stages):
+        for stream in heavy:
+            sums.advance(stream, stage)
+    for step in range(1, owners):
+        source = lax.rem(mine + owners - step, owners)
+        share_copy(source, source, step).wait_recv()
+    spread = Spread(dims, streams[light]["order"], whole, gather_send, gather_recv)
+    for step in range(len(tok_dims)):
+        spread.start()
+        if step == 0:
+            for stream in slices:
+                sums.advance(stream, 1)
+        spread.finish()
+    for copy in moves + shares:
+        copy.wait_send()
+    unpack_blocks(blocks, whole, wide_out, stages)
+
+    @pl.loop(0, depth * 2)
+    def _(image):
+        pixel_local(image).wait()
+
+        @pl.loop(1, owners)
+        def _(step):
+            source = lax.rem(mine + owners - step, owners)
+            pltpu.make_async_remote_copy(
+                src_ref=pix_ref.at[source, image],
+                dst_ref=pixel_land.at[source, image],
+                send_sem=pixel_send.at[image, step - 1],
+                recv_sem=pixel_recv.at[image, step - 1],
+                device_id=at_band(source),
+                device_id_type=MESH,
+            ).wait()
+
+    for copy in copies + [near] + far + [relay(step) for step in range(1, depth)]:
+        copy.wait_send()
+    sums.drain()
+
+
+def tail_call(
+    gen_grid,
+    pix,
+    low_own,
+    even,
+    odd,
+    weights,
+    features,
+    token,
+    bias_grad,
+    params,
+    gen_b_grad,
+    gain_lines,
+    factor,
+    collective_id,
+):
+    dims, band_bits, tok_bits = mesh_bits()
+    everything = len(dims)
+    low = jnp.bfloat16
+    owners, images, share, slot = pix.shape
+    depth = owners // 2
+    pixel_share, model_dim, hyper_dim = gen_grid.shape
+    rows = owners * 8
+    split, outs, landing, streams = [], [], [], []
+    order = halving_order(0, band_bits, tok_bits)
+    tallest = 0
+    for k, weight in enumerate(weights):
+        height = weight.shape[0] >> everything
+        split.append(weight.reshape((2,) * everything + (height, weight.shape[1])))
+        outs.append(jax.ShapeDtypeStruct((height, weight.shape[1]), jnp.float32))
+        for start, size in row_chunks(height, 2 if height > 32 else 1):
+            streams.append(stream_entry(k, k, start, size, order, dims, True))
+            landing += landing_shapes(streams[-1], weight.shape[1])
+            tallest = max(tallest, size)
+    bulk = len(weights)
+    tok_order = halving_order(2, band_bits, tok_bits)
+    height = pixel_share * model_dim >> tok_bits
+    outs.append(jax.ShapeDtypeStruct((height, hyper_dim), jnp.float32))
+    for start, size in row_chunks(height, 4):
+        out_rows = size
+        streams.append(stream_entry(bulk, bulk, start, size, tok_order, dims, False, factor))
+        landing += landing_shapes(streams[-1], hyper_dim)
+    wide_shapes = [p.shape for p in params[:6]] + [gen_b_grad.shape, gain_lines.shape]
+    blocks, used, piece = wide_plan(wide_shapes, 1 << everything)
+    light = stream_entry(bulk + 1, None, 0, piece, tok_order, dims, False)
+    light["span"] = dims
+    streams.append(light)
+    landing += [
+        pltpu.VMEM((2,) * (everything - 1 - stage) + (piece, 128), low)
+        for stage in range(tok_bits)
+    ]
+    count = len(streams)
+    plan = {"streams": streams, "dims": dims, "bulk": bulk, "blocks": blocks, "used": used}
+    space = (2,) * everything + (piece, 128)
+    own = pltpu.VMEM((2,) * (everything - 1) + (tallest, model_dim), low)
+    dma = pltpu.SemaphoreType.DMA
+    return pl.pallas_call(
+        functools.partial(tail_kernel, factor, plan),
+        out_shape=[jax.ShapeDtypeStruct(pix.shape, low)]
+        + outs
+        + [jax.ShapeDtypeStruct(shape, jnp.float32) for shape in wide_shapes],
+        in_specs=[pl.BlockSpec(memory_space=pl.ANY)] * (2 + bulk)
+        + [pl.BlockSpec(memory_space=pltpu.VMEM)] * 10
+        + [pl.BlockSpec(memory_space=pl.ANY)] * 2
+        + [pl.BlockSpec(memory_space=pltpu.VMEM)] * 4,
+        out_specs=[pl.BlockSpec(memory_space=pl.ANY)]
+        + [pl.BlockSpec(memory_space=pltpu.VMEM)] * bulk
+        + [pl.BlockSpec(memory_space=pl.ANY)]
+        + [pl.BlockSpec(memory_space=pltpu.VMEM)] * len(wide_shapes),
+        scratch_shapes=[
+            pltpu.VMEM(gen_grid.shape, low),
+            pltpu.VMEM(pix.shape, low),
+            pltpu.VMEM((images // 2, 2, owners, share, model_dim), low),
+            pltpu.VMEM((images, slot, model_dim), low),
+            pltpu.VMEM((2, owners, share, slot), low),
+            pltpu.VMEM((2, depth, rows, hyper_dim), jnp.float32),
+            pltpu.VMEM((owners - 1, 2, rows, hyper_dim), jnp.float32),
+            pltpu.VMEM((features.shape[0] + 8, hyper_dim), jnp.float32),
+            own,
+            own,
+        ]
+        + landing
+        + [
+            pltpu.VMEM(space, low),
+            pltpu.VMEM(space, low),
+            dma((4,)),
+            dma,
+            dma((depth - 1,)),
+            dma((depth - 1,)),
+            dma((owners,)),
+            dma((owners - 1,)),
+            dma((owners - 1,)),
+            dma((count, everything)),
+            dma((count, everything)),
+            dma((2,)),
+            dma((everything,)),
+            dma((everything,)),
+            dma((images, owners - 1)),
+            dma((images, owners - 1)),
+            dma((images,)),
+            pltpu.VMEM((owners - 1, piece, 128), low),
+            dma((owners - 1,)),
+            dma((owners - 1,)),
+            dma((owners - 1,)),
+            dma((owners - 1,)),
+            pltpu.VMEM((out_rows, hyper_dim), jnp.float32),
+            dma,
+        ],
+        compiler_params=pltpu.CompilerParams(
+            collective_id=collective_id, has_side_effects=True, vmem_limit_bytes=63 << 20
+        ),
+        cost_estimate=pl.CostEstimate(
+            flops=2 * 10**10, bytes_accessed=3 * 10**8, transcendentals=0
+        ),
+    )(
+        gen_grid,
+        pix,
+        *split,
+        low_own,
+        even,
+        odd,
+        features,
+        token,
+        bias_grad,
+        *params,
+        gen_b_grad,
+        gain_lines,
+    )
 
 
 def layer_norm(values, scaling, epsilon):
@@ -84,6 +1175,71 @@
         EPS_HYPER,
     )
     return (second[:, :-1, :], second[:, -1, :])
+
+
+def precise_dot(left, right, contract=(1, 0)):
+    return lax.dot_general(
+        left,
+        right,
+        (((contract[0],), (contract[1],)), ((), ())),
+        precision=PRECISE,
+        preferred_element_type=jnp.float32,
+    )
+
+
+def hyper_attention(tokens, params, images):
+    query, key, value, mix, first = params
+    rows, hyper_dim = tokens.shape
+    bands = (rows - 8 * -(-images // 8)) // images
+    head = hyper_dim // HHEADS
+
+    def owner(index):
+        return jnp.where(index < images * bands, lax.div(index, bands), index - images * bands)
+
+    same = owner(lax.broadcasted_iota(jnp.int32, (rows, rows), 0)) == owner(
+        lax.broadcasted_iota(jnp.int32, (rows, rows), 1)
+    )
+    lane = lax.div(lax.broadcasted_iota(jnp.int32, (1, hyper_dim), 1), head)
+    queries = precise_dot(tokens, query) * (1.0 / math.sqrt(head))
+    keys_all = precise_dot(tokens, key)
+    values_all = precise_dot(tokens, value)
+    blended = None
+    for place in range(HHEADS):
+        chosen = (lane == place).astype(jnp.float32)
+        scores = precise_dot(queries * chosen, keys_all, (1, 1))
+        scores = jnp.where(same, scores, -1e30)
+        highest = lax.stop_gradient(jnp.max(scores, axis=-1, keepdims=True))
+        lifted = jnp.exp(scores - highest)
+        weights = lifted / jnp.sum(lifted, axis=-1, keepdims=True)
+        part = precise_dot(weights, values_all * chosen)
+        blended = part if blended is None else blended + part
+    return layer_norm(tokens + precise_dot(blended, mix), first, EPS_HYPER)
+
+
+def hyper_wide(segment, expand_ref, shrink_ref, total_ref, width):
+    total_ref[...] = segment
+
+    @pl.loop(0, expand_ref.shape[1] // width)
+    def _(part):
+        columns = pl.ds(pl.multiple_of(part * width, width), width)
+        wide = precise_dot(segment, expand_ref[:, columns])
+        active = 0.5 * wide * (1.0 + lax.erf(wide * math.sqrt(0.5)))
+        total_ref[...] += precise_dot(active, shrink_ref[columns, :])
+
+
+def hyper_wide_back(segment, d_total, expand_ref, shrink_ref, d_segment_ref, width):
+    d_segment_ref[...] = d_total
+
+    @pl.loop(0, expand_ref.shape[1] // width)
+    def _(part):
+        columns = pl.ds(pl.multiple_of(part * width, width), width)
+        wide = precise_dot(segment, expand_ref[:, columns])
+        bell = 0.5 * (1.0 + lax.erf(wide * math.sqrt(0.5)))
+        slope = bell + wide * jnp.exp(-0.5 * wide * wide) * (1.0 / math.sqrt(2.0 * math.pi))
+        d_wide = precise_dot(d_total, shrink_ref[columns, :], (1, 1)) * slope
+        d_segment_ref[...] += precise_dot(d_wide, expand_ref[:, columns], (1, 1))
+        shrink_ref[columns, :] = precise_dot(wide * bell, d_total, (0, 0))
+        expand_ref[:, columns] = precise_dot(segment, d_wide, (0, 0))
 
 
 def contract_rows(left_side, right_side):
@@ -262,13 +1418,23 @@
         hyper_gain1,
         hyper_gain2,
     )
-    pixel_turned = pixels[0].reshape(
-        group_images, band_share, slot_count, owners, slice_pixels
-    ).transpose(3, 0, 4, 1, 2)
-    pixel_slices = lax.all_to_all(pixel_turned, "band", 0, 0, tiled=True)
-    pixel_slices = pixel_slices.transpose(1, 2, 0, 3, 4).reshape(
-        group_images, slice_pixels * all_bands, slot_count
-    )
+    paired = (
+        band_share == 4
+        and own_images == 1
+        and group_images == owners
+        and owners % 2 == 0
+        and slice_pixels % 4 == 0
+        and model_dim % 256 == 0
+    )
+    if paired:
+        pixel_lined = lax.all_to_all(turn_pixels(pixels[0], owners), "band", 0, 0, tiled=True)
+    else:
+        pixel_turned = (
+            pixels[0]
+            .reshape(group_images, band_share, slot_count, owners, slice_pixels)
+            .transpose(3, 0, 4, 1, 2)
+        )
+        pixel_blocks = lax.all_to_all(pixel_turned, "band", 0, 0, tiled=True)
     gen_part = lax.all_gather(gen_w, "tok", axis=0, tiled=True)
     gen_grid = gen_part.reshape(slice_pixels, model_dim, hyper_dim)
     weights_full = (
@@ -289,22 +1455,37 @@
         return hyper_layer(own_input, params)
 
     (_, bias_own), hyper_back = jax.vjp(run_hyper, hyper_params)
-    kernels = (
-        jnp.einsum("pdc,nc->pnd", gen_grid, band_low, preferred_element_type=jnp.float32) * factor
-    ).astype(jnp.bfloat16)
-    kernel_grid = kernels.reshape(slice_pixels, group_images, all_bands, model_dim)
-    kernel_rows = kernel_grid.transpose(1, 0, 2, 3).reshape(
-        group_images, slice_pixels * all_bands, model_dim
-    )
-    product = jnp.einsum(
-        "iks,ikd->isd", pixel_slices, kernel_rows, preferred_element_type=jnp.float32
-    )
-    convolved = lax.psum_scatter(
-        product.reshape(group_images * slot_count, model_dim).astype(jnp.bfloat16),
-        "band",
-        scatter_dimension=0,
-        tiled=True,
-    ).astype(jnp.float32)
+    if paired:
+        ordered = (
+            band_feats.astype(jnp.bfloat16)
+            .reshape(group_images // 2, 2, owners, band_share, hyper_dim)
+            .transpose(0, 2, 1, 3, 4)
+        )
+        even_rows = ordered.reshape(-1, hyper_dim)
+        odd_rows = ordered[:, :, ::-1].reshape(-1, hyper_dim)
+        convolved = embed_parts(
+            gen_grid, pixel_lined, even_rows, odd_rows, model_dim, factor, 1
+        )
+    else:
+        pixel_slices = pixel_blocks.transpose(1, 2, 0, 3, 4).reshape(
+            group_images, slice_pixels * all_bands, slot_count
+        )
+        kernels = (
+            jnp.einsum("pdc,nc->pnd", gen_grid, band_low, preferred_element_type=jnp.float32) * factor
+        ).astype(jnp.bfloat16)
+        kernel_grid = kernels.reshape(slice_pixels, group_images, all_bands, model_dim)
+        kernel_rows = kernel_grid.transpose(1, 0, 2, 3).reshape(
+            group_images, slice_pixels * all_bands, model_dim
+        )
+        product = jnp.einsum(
+            "iks,ikd->isd", pixel_slices, kernel_rows, preferred_element_type=jnp.float32
+        )
+        convolved = lax.psum_scatter(
+            product.reshape(group_images * slot_count, model_dim).astype(jnp.bfloat16),
+            "band",
+            scatter_dimension=0,
+            tiled=True,
+        ).astype(jnp.float32)
     bias_rows = jnp.dot(bias_own, gen_b, precision=PRECISE)
     embedded = convolved.reshape(own_images, slot_count, model_dim) + bias_rows[:, None, :]
     usable = lax.broadcasted_iota(jnp.int32, (own_images, slot_count), 1) < patch_count[0][:, None]
@@ -323,63 +1504,82 @@
     d_bias = jnp.sum(d_embed.reshape(own_images, slot_count, model_dim), axis=1)
     d_bias_feat = jnp.dot(d_bias, gen_b.T, precision=PRECISE)
     grad_gen_b = jnp.dot(bias_own.T, d_bias, precision=PRECISE)
-    d_gathered = lax.all_gather(d_embed_low, "band", axis=0, tiled=True)
-    grad_slices = jnp.einsum(
-        "ikd,isd->iks", kernel_rows, d_gathered, preferred_element_type=jnp.float32
-    ).astype(jnp.bfloat16)
-    grad_slices = grad_slices.reshape(
-        group_images, slice_pixels, owners, band_share, slot_count
-    ).transpose(2, 0, 1, 3, 4)
-    grad_slices = lax.all_to_all(grad_slices, "band", 0, 0, tiled=True)
-    pixel_grad = grad_slices.transpose(1, 3, 4, 0, 2).reshape(pixels.shape)
-    d_kernel = jnp.einsum(
-        "iks,isd->ikd", pixel_slices, d_gathered, preferred_element_type=jnp.float32
-    ).astype(jnp.bfloat16)
-    d_kernel = (
-        d_kernel.reshape(group_images, slice_pixels, all_bands, model_dim)
-        .transpose(1, 0, 2, 3)
-        .reshape(slice_pixels, group_images * all_bands, model_dim)
-    )
-    d_band_part = (
-        jnp.einsum("pnd,pdc->nc", d_kernel, gen_grid, preferred_element_type=jnp.float32) * factor
-    )
-    d_band_own = lax.psum_scatter(d_band_part, "band", scatter_dimension=0, tiled=True)
-    gen_part_grad = (
-        jnp.einsum("pnd,nc->pdc", d_kernel, band_low, preferred_element_type=jnp.float32) * factor
-    )
-    grad_gen_w = lax.psum_scatter(
-        gen_part_grad.reshape(-1, hyper_dim).astype(jnp.bfloat16),
-        "tok",
-        scatter_dimension=0,
-        tiled=True,
-    ).astype(jnp.float32)
-    (
-        grad_token,
-        grad_query,
-        grad_key,
-        grad_value,
-        grad_mix,
-        grad_expand,
-        grad_shrink,
-        grad_first_gain,
-        grad_second_gain,
-    ) = hyper_back((d_band_own.reshape(own_images, all_bands, hyper_dim), d_bias_feat))[0]
     qkv_turned, out_turned, up_turned, grad_down, gain_one, gain_two = block_terms
-
-    def spread(term):
-        return lax.psum_scatter(
-            term.astype(jnp.bfloat16), ("band", "tok"), scatter_dimension=0, tiled=True
-        ).astype(jnp.float32)
-
-    block_sums = (
-        spread(qkv_turned),
-        spread(out_turned),
-        spread(up_turned),
-        spread(grad_down),
-        lax.psum_scatter(gain_one, ("band", "tok"), scatter_dimension=0, tiled=True),
-        lax.psum_scatter(gain_two, ("band", "tok"), scatter_dimension=0, tiled=True),
-    )
-    hyper_sums = lax.psum(
+    weight_terms = [
+        term.astype(jnp.bfloat16) for term in (qkv_turned, out_turned, up_turned, grad_down)
+    ]
+    gain_rows = model_dim // hyper_dim
+    gain_lines = [gain_one.reshape(-1, hyper_dim), gain_two.reshape(-1, hyper_dim)]
+    fill = -(3 + 2 * gain_rows) % 16
+    gain_lines.append(jnp.zeros((fill, hyper_dim), jnp.float32))
+    if paired:
+        (
+            grad_blocks,
+            qkv_sum,
+            out_sum,
+            up_sum,
+            down_sum,
+            grad_gen_w,
+            query_sum,
+            key_sum,
+            value_sum,
+            mix_sum,
+            expand_sum,
+            shrink_sum,
+            gen_b_sum,
+            line_sum,
+        ) = tail_call(
+            gen_grid,
+            pixel_lined,
+            d_embed_low.reshape(slot_count, model_dim),
+            even_rows,
+            odd_rows,
+            weight_terms,
+            own_input[0],
+            bias_token[None],
+            d_bias_feat,
+            [
+                hyper_query,
+                hyper_key,
+                hyper_value,
+                hyper_out,
+                hyper_up,
+                hyper_down,
+                hyper_gain1[None],
+                hyper_gain2[None],
+            ],
+            grad_gen_b,
+            jnp.concatenate([jnp.zeros((3, hyper_dim), jnp.float32)] + gain_lines),
+            factor,
+            2,
+        )
+        pixel_grad = unturn_pixels(grad_blocks, pixels.shape[1:])[None]
+    else:
+        d_gathered = lax.all_gather(d_embed_low, "band", axis=0, tiled=True)
+        grad_slices = jnp.einsum(
+            "ikd,isd->iks", kernel_rows, d_gathered, preferred_element_type=jnp.float32
+        ).astype(jnp.bfloat16)
+        grad_slices = grad_slices.reshape(
+            group_images, slice_pixels, owners, band_share, slot_count
+        ).transpose(2, 0, 1, 3, 4)
+        d_kernel = jnp.einsum(
+            "iks,isd->ikd", pixel_slices, d_gathered, preferred_element_type=jnp.float32
+        ).astype(jnp.bfloat16)
+        d_kernel = (
+            d_kernel.reshape(group_images, slice_pixels, all_bands, model_dim)
+            .transpose(1, 0, 2, 3)
+            .reshape(slice_pixels, group_images * all_bands, model_dim)
+        )
+        d_band_part = (
+            jnp.einsum("pnd,pdc->nc", d_kernel, gen_grid, preferred_element_type=jnp.float32) * factor
+        )
+        d_band_own = lax.psum_scatter(d_band_part, "band", scatter_dimension=0, tiled=True)
+        gen_part_grad = (
+            jnp.einsum("pnd,nc->pdc", d_kernel, band_low, preferred_element_type=jnp.float32) * factor
+        )
+        gen_low = gen_part_grad.reshape(-1, hyper_dim).astype(jnp.bfloat16)
+        grad_slices = lax.all_to_all(grad_slices, "band", 0, 0, tiled=True)
+        pixel_grad = grad_slices.transpose(1, 3, 4, 0, 2).reshape(pixels.shape)
         (
             grad_token,
             grad_query,
@@ -390,30 +1590,67 @@
             grad_shrink,
             grad_first_gain,
             grad_second_gain,
-            grad_gen_b,
-        ),
-        ("band", "tok"),
-    )
+        ) = hyper_back((d_band_own.reshape(own_images, all_bands, hyper_dim), d_bias_feat))[0]
+        lines = jnp.concatenate(
+            [grad_token[None], grad_first_gain[None], grad_second_gain[None]] + gain_lines
+        )
+        (
+            qkv_sum,
+            out_sum,
+            up_sum,
+            down_sum,
+            grad_gen_w,
+            query_sum,
+            key_sum,
+            value_sum,
+            mix_sum,
+            expand_sum,
+            shrink_sum,
+            gen_b_sum,
+            line_sum,
+        ) = reduce_all(
+            weight_terms + [gen_low],
+            [1, 0, 1, 1, 2],
+            [2, 1, 2, 2, 2],
+            [
+                grad_query,
+                grad_key,
+                grad_value,
+                grad_mix,
+                grad_expand,
+                grad_shrink,
+                grad_gen_b,
+                lines,
+            ],
+            3,
+        )
+    devices = owners * lax.axis_size("tok")
+    place = band_place * lax.axis_size("tok") + lax.axis_index("tok")
+    gain_share = model_dim // devices
+
+    def own_gain(whole):
+        return lax.dynamic_slice_in_dim(whole.reshape(-1), place * gain_share, gain_share, 0)
+
     return (
         layer_out,
         pixel_grad,
         grad_gen_w,
-        hyper_sums[9],
-        hyper_sums[0],
-        hyper_sums[1],
-        hyper_sums[2],
-        hyper_sums[3],
-        hyper_sums[4],
-        hyper_sums[5],
-        hyper_sums[6],
-        hyper_sums[7],
-        hyper_sums[8],
-        block_sums[0].T,
-        block_sums[1].T,
-        block_sums[2].T,
-        block_sums[3],
-        block_sums[4],
-        block_sums[5],
+        gen_b_sum,
+        line_sum[0],
+        query_sum,
+        key_sum,
+        value_sum,
+        mix_sum,
+        expand_sum,
+        shrink_sum,
+        line_sum[1],
+        line_sum[2],
+        qkv_sum.T,
+        out_sum.T,
+        up_sum.T,
+        down_sum,
+        own_gain(line_sum[3 : 3 + gain_rows]),
+        own_gain(line_sum[3 + gain_rows : 3 + 2 * gain_rows]),
     )
 
 

time: 1240 us -> 499 us (0.40)
  waiting for transfers between devices: 875 us -> 60.7 us
  Pallas kernels: 0 us -> 275 us
  local copies, waits for them, and re-layouts: 104 us -> 29.9 us
  matrix products: 151 us -> 89 us
  blocking collectives: 40.1 us -> 0 us
  other arithmetic: 27.4 us -> 12.2 us
    reduce_scatter x7 -> x0, waiting for transfers between devices: 494 us -> none  [the longest x4 382 us: spread(): lax.psum_scatter(term.astype(jnp.bfloat16), ('band', 'tok'), scatter_dime...]
    pallas_call x0 -> x4, Pallas kernels: none -> 275 us  [the longest x1 210 us: tail_call(): pl.pallas_call(functools.partial(tail_kernel, factor, plan), out_shape=[j...]
    psum x1 -> x0, waiting for transfers between devices: 145 us -> none  [body(): lax.psum((grad_token, grad_query, grad_key, grad_value, grad_mix, grad_ex...]
    all_gather x1 -> x0, waiting for transfers between devices: 60.4 us -> none  [body(): d_gathered = lax.all_gather(d_embed_low, 'band', axis=0, tiled=True)]
    dot_general x6 -> x0, matrix products: 57 us -> none  [the longest x1 11.6 us: body(): jnp.einsum('iks,isd->ikd', pixel_slices, d_gathered, preferred_element_ty...]
    psum x1 -> x0, blocking collectives: 40.1 us -> none  [body(): lax.psum((grad_token, grad_query, grad_key, grad_value, grad_mix, grad_ex...]
    all_gather x1, waiting for transfers between devices: 36.6 us -> 0.02 us  [body(): lax.all_gather(w_up, 'tok', axis=1, tiled=True)]
    all_gather x1, waiting for transfers between devices: 29.1 us -> 0.02 us  [body(): lax.all_gather(w_qkv, 'tok', axis=1, tiled=True)]
  transfers between devices with their start and end apart: 16 -> 6, of which waited for: 13 -> 1; matrix products, arithmetic and copies ran while one was open for 14% -> 14% of each run, Pallas kernels for 0% -> 12%
where the time goes in v2:
time: 499 us; the launch traced here: 490 us
  Pallas kernels  275 us (55%)
  matrix products  89 us (18%)
  waiting for transfers between devices  60.7 us (12%)
  local copies, waits for them, and re-layouts  29.9 us (6%)
  between operations  15.9 us (3%)
  other arithmetic  12.2 us (2%)
  starting transfers between devices  7.62 us (2%)
    pallas_call x1, Pallas kernels, tail_call(): pl.pallas_call(functools.partial(tail_kernel, factor, plan), out_shape=[j...  210 us
    all_to_all x1, waiting for transfers between devices, body(): lax.all_to_all(turn_pixels(pixels[0], owners), 'band', 0, 0, tiled=True)  57.5 us
    pallas_call x1, Pallas kernels, embed_parts(): pl.pallas_call(functools.partial(embed_kernel, factor), out_shape=jax.Sha...  56.8 us
    unnamed x161, local copies, waits for them, and re-layouts  20.3 us
    dot_general x1, matrix products, block_forward(): hidden = jnp.dot(normed_two, w_up_full, preferred_element_type=jnp.float32)  20.1 us
    dot_general x2, matrix products, hyper_layer(): jnp.einsum('nsf,fe->nse', expanded, hyper_down, precision=PRECISE)  14.6 us
    dot_general x4, matrix products, contract_rows(): lax.dot_general(left_side, right_side, (((0,), (0,)), ((), ())), preferre...  11.9 us
    dot_general x4, matrix products, contract_cols(): lax.dot_general(left_side, right_side, (((1,), (1,)), ((), ())), preferre...  11.1 us
  transfers between devices with their start and end apart: 6, of which 1 were waited for; matrix products, arithmetic and copies ran while one was open for 14% of the time, Pallas kernels for 12%

profile of v2, /device:TPU:0, one launch (start us, length us, event | category | flops | bytes accessed | tf_op | source)
XLA Modules:
  0.0 490.1 jit_solution(13494255880428670798)
XLA Ops:
  7.2 0.7 all-gather.6.cloned.1.call-update
  8.0 0.7 all-gather.8.cloned.1.call-update
  8.7 0.7 all-gather.10.cloned.1.call-update
  10.0 2.2 copy-done.2
  12.2 2.9 shard_map.357
  15.1 2.0 copy-done.1
  17.1 7.4 %all-to-all-start = ((bf16[8,8,128,256]{3,2,1,0:T(8,128)(2,1)}), bf16[8,8,128,256]{3,2,1,0:T(8,128)(2,1)}, u32[]{:S(2)}, u32[]{:S(2)}) async-start(bf16[8,8,128,256]{3,2,1,0:T(8,128)(2,1)} %copy-done.1), calls=%async_computation | async-start | bytes 8388608 | tf_op jit(solution)/shard_map/all_to_all | solution.py:1430
  27.9 1.4 fusion.323
  29.4 0.8 fusion.119
  30.3 1.1 fusion.324
  31.6 5.1 %fusion.123 = (u8[33,2048]{1,0:T(8,128)(4,1)S(1)}, u8[33,2048]{1,0:T(8,128)(4,1)S(1)}, u8[33,2048]{1,0:T(8,128)(4,1)S(1)}, f32[8,33,2048]{2,1,0:T(8,128)}) fusion(f32[128,2048]{1,0:T(8,128)S(1)} %copy-done.19, f32[8,33,128]{2,1,0:T(8,128)S(1)} %get-tuple-element.76, f32[128]{0:T(128)S(1)} %copy-done.66, f32[8,33]{1,0:T(8,128)S(1)} %add_rsqrt_fusion.1, ...), kind=kOutput, calls=%fused_computation.178 | convolution fusion | flops 841184256 | bytes 3551808 | tf_op jit(solution)/shard_map/nse,ef->nsf/dot_general | solution.py:1170
  39.3 1.0 and_convert_fusion
  40.3 11.9 %fusion.325 = (f32[8,33]{1,0:T(8,128)S(1)}, f32[8,33,128]{2,1,0:T(8,128)S(1)}) fusion(f32[2048,128]{1,0:T(8,128)} %refs_17_.1, pred[8,33,2048]{2,1,0:T(8,128)(4,1)S(1)} %and_convert_fusion.2, pred[8,33,2048]{2,1,0:T(8,128)(4,1)S(1)} %get-tuple-element.96, pred[8,33,2048]{2,1,0:T(8,128)(4,1)S(1)} %get-tuple-element.95, ...), kind=kOutput, calls=%fused_computation.430 | convolution fusion | flops 863621888 | bytes 5107296 | tf_op jit(solution)/shard_map/nsf,fe->nse/dot_general | solution.py:1173
  52.6 0.7 rev.3
  55.7 0.7 fusion.242
  56.4 2.7 fusion.328
  60.3 57.5 %all-to-all-done.pix_hbm.refs_1_ = bf16[8,8,128,256]{3,2,1,0:T(8,128)(2,1)} async-done(((bf16[8,8,128,256]{3,2,1,0:T(8,128)(2,1)}), bf16[8,8,128,256]{3,2,1,0:T(8,128)(2,1)}, u32[]{:S(2)}, u32[]{:S(2)}) %all-to-all-start) | async-done | bytes 4194336 | tf_op jit(solution)/shard_map/all_to_all | solution.py:1430
  117.8 56.8 %shard_map.358 = f32[256,768]{1,0:T(8,128)} custom-call(bf16[32,768,128]{2,1,0:T(8,128)(2,1)} %bitcast.240, bf16[8,8,128,256]{3,2,1,0:T(8,128)(2,1)} %all-to-all-done.pix_hbm.refs_1_, bf16[256,128]{1,0:T(8,128)(2,1)} %bitcast.219, bf16[256,128]{1,0:T(8,128)(2,1)} %bitcast.226), custom_call_target="tpu_custom_call" | custom-call | flops 10000000000 | bytes 120000000 | tf_op jit(solution)/shard_map/pallas_call | solution.py:576
  174.6 1.3 add_reduce_fusion
  175.9 1.4 multiply_reduce_fusion.6
  177.4 3.5 convolution_convert_fusion.3
  180.9 1.4 copy.89
  182.3 1.9 fusion.329
  184.8 0.6 copy-done.37
  185.4 2.4 fusion.98
  187.9 2.2 fusion.330
  190.1 0.8 copy-done.5
  191.8 20.1 %multiply_convert_fusion.1 = (bf16[256,3072]{1,0:T(8,128)(2,1)}, f32[256,3072]{1,0:T(8,128)}, f32[256,3072]{1,0:T(8,128)}) fusion(bf16[768,3072]{1,0:T(8,128)(2,1)} %all-gather.12.cloned.1.call-done, f32[256,768]{1,0:T(8,128)} %copy-done.5, f32[768]{0:T(1024)} %param.43, f32[256]{0:T(256)} %fusion.251, f32[256]{0:T(256)} %copy-done.48), kind=kOutput, calls=%fused_computation.11 | convolution fusion | flops 1259864064 | bytes 13374464 | tf_op jit(solution)/shard_map/dot_general | solution.py:1292
  212.0 6.3 %add_convert_fusion = bf16[256,3072]{1,0:T(8,128)(2,1)S(1)} fusion(f32[256,3072]{1,0:T(8,128)} %get-tuple-element.61, f32[256,3072]{1,0:T(8,128)} %get-tuple-element.90, bf16[3072,768]{1,0:T(8,128)(2,1)} %all-gather.14.cloned.1.call-done, bf16[1,1,256,768]{3,2,1,0:T(8,128)(2,1)} %param.26, pred[256]{0:T(512)(128)(4,1)} %iota_compare_fusion.1), kind=kOutput, calls=%fused_computation.9 | convolution fusion | flops 1219559424 | bytes 12976384 | tf_op jit(solution)/shard_map/dot_general | solution.py:1252
  218.4 3.8 convolution_convert_fusion.1
  222.2 2.2 multiply_reduce_fusion.1
  224.8 0.9 copy-done.9
  225.8 1.5 convolution_convert_fusion.4
  227.4 1.2 convolution_convert_fusion.5
  228.6 1.9 copy.91
  230.5 1.7 fusion.108
  232.3 0.8 multiply_reduce_fusion
  233.1 0.7 multiply_convert_fusion
  235.6 3.0 convolution_convert_fusion.2
  238.6 1.3 multiply_reduce_fusion.2
  240.4 0.7 copy-done.10
  241.2 1.0 fusion.319
  242.2 1.1 fusion.331.refs_11_
  243.3 0.8 broadcast_multiply_fusion.refs_20_
  244.2 3.6 convolution_convert_fusion
  247.8 0.7 maximum_maximum_fusion.refs_21_
  248.5 210.2 %shard_map.359 = (bf16[8,8,128,256]{3,2,1,0:T(8,128)(2,1)}, f32[72,768]{1,0:T(8,128)}, f32[24,768]{1,0:T(8,128)}, f32[96,768]{1,0:T(8,128)}, f32[96,768]{1,0:T(8...) custom-call(bf16[32,768,128]{2,1,0:T(8,128)(2,1)} %bitcast.241, ...), custom_call_target="tpu_custom_call" | custom-call | flops 20000000000 | bytes 300000000 | tf_op jit(solution)/shard_map/pallas_call | solution.py:1034
  458.7 1.3 slice_bitcast_fusion.11
  460.0 0.8 slice_bitcast_fusion.9
  460.8 2.2 copy-done.3
  463.0 4.7 shard_map.360
  468.8 4.6 fusion.105
  473.5 1.7 copy.131
  475.2 0.7 copy.132
  475.9 0.6 copy.133
  476.6 0.6 copy.134
  477.2 0.6 copy.135
  477.8 0.6 copy.136
  478.5 1.0 copy.137
  479.4 1.0 copy.138
  480.4 0.7 copy.139
  481.1 0.6 copy.140
  481.7 0.7 copy.141
  482.4 0.7 copy.142
  (217 shorter events, 15.5 us)
Async XLA Ops:
  7.2 52.2 %copy-start = (f32[128,768]{1,0:T(8,128)S(1)}, f32[128,768]{1,0:T(8,128)}, u32[]{:S(2)}) copy-start(f32[128,768]{1,0:T(8,128)} %param.28) | copy-start | bytes 1179652
  7.2 110.6 %all-gather.6.cloned.1.call-start = ((), (), s32[]{:S(2)}) async-start(), calls=%async_computation.1 | async-start | bytes 7864320 | tf_op jit(solution)/shard_map/all_gather | solution.py:1438
  7.9 169.4 %all-gather.8.cloned.1.call-start = ((), (), s32[]{:S(2)}) async-start(), calls=%async_computation.2 | async-start | bytes 4423680 | tf_op jit(solution)/shard_map/all_gather | solution.py:1441
  8.7 179.2 %all-gather.10.cloned.1.call-start = ((), (), s32[]{:S(2)}) async-start(), calls=%async_computation.3 | async-start | bytes 1474560 | tf_op jit(solution)/shard_map/all_gather | solution.py:1442
  9.4 182.4 %all-gather.12.cloned.1.call-start = ((), (), s32[]{:S(2)}) async-start(), calls=%async_computation.4 | async-start | bytes 5898240 | tf_op jit(solution)/shard_map/all_gather | solution.py:1443
  10.0 2.2 copy-start.2
  15.1 2.0 copy-start.1
  17.1 8.1 %copy-start.64 = (s32[1,8,32]{2,1,0:T(8,128)S(1)}, s32[1,8,32]{2,1,0:T(8,128)}, u32[]{:S(2)}) copy-start(s32[1,8,32]{2,1,0:T(8,128)} %param.24) | copy-start | bytes 3076
  17.1 8.1 %copy-start.68 = (f32[64]{0:T(128)S(1)}, f32[64]{0:T(128)}, u32[]{:S(2)}) copy-start(f32[64]{0:T(128)} %param.23) | copy-start | bytes 772
  17.1 8.8 %copy-start.50 = (f32[128]{0:T(128)S(1)}, f32[128]{0:T(128)}, u32[]{:S(2)}) copy-start(f32[128]{0:T(128)} %param.29) | copy-start | bytes 1540
  17.1 8.9 %copy-start.29 = (f32[128,128]{1,0:T(8,128)S(1)}, f32[128,128]{1,0:T(8,128)}, u32[]{:S(2)}) copy-start(f32[128,128]{1,0:T(8,128)} %refs_12_.1) | copy-start | bytes 196612
  17.1 9.3 %copy-start.30 = (f32[128,128]{1,0:T(8,128)S(1)}, f32[128,128]{1,0:T(8,128)}, u32[]{:S(2)}) copy-start(f32[128,128]{1,0:T(8,128)} %refs_13_.1) | copy-start | bytes 196612
  17.1 100.7 %all-to-all-start = ((bf16[8,8,128,256]{3,2,1,0:T(8,128)(2,1)}), bf16[8,8,128,256]{3,2,1,0:T(8,128)(2,1)}, u32[]{:S(2)}, u32[]{:S(2)}) async-start(bf16[8,8,128,256]{3,2,1,0:T(8,128)(2,1)} %copy-done.1), calls=%async_computation | async-start | bytes 8388608 | tf_op jit(solution)/shard_map/all_to_all | solution.py:1430
  24.5 2.3 copy-start.28
  24.5 187.4 %all-gather.14.cloned.1.call-start = ((), (), s32[]{:S(2)}) async-start(), calls=%async_computation.5 | async-start | bytes 5898240 | tf_op jit(solution)/shard_map/all_gather | solution.py:1444
  27.9 2.4 copy-start.26
  29.3 2.3 copy-start.19
  29.3 2.3 copy-start.66
  40.3 12.2 %copy-start.65 = (f32[128]{0:T(128)S(1)}, f32[128]{0:T(128)}, u32[]{:S(2)}) copy-start(f32[128]{0:T(128)} %param.37) | copy-start | bytes 1540
  52.6 6.5 %copy-start.27 = (bf16[4,2,8,4,128]{4,3,1,2,0:T(4,128)(2,1)}, bf16[4,2,8,4,128]{4,3,1,2,0:T(4,128)(2,1)S(1)}, u32[]{:S(2)}) copy-start(bf16[4,2,8,4,128]{4,3,1,2,0:T(4,128)(2,1)S(1)} %copy.117) | copy-start | bytes 196612
  53.9 5.2 %copy-start.22 = (f32[1,32,128]{2,1,0:T(8,128)}, f32[1,32,128]{2,1,0:T(8,128)S(1)}, u32[]{:S(2)}) copy-start(f32[1,32,128]{2,1,0:T(8,128)S(1)} %fusion.246) | copy-start | bytes 49156
  59.7 128.1 %copy-start.32 = (f32[768]{0:T(1024)}, f32[768]{0:T(1024)S(1)}, u32[]{:S(2)}) copy-start(f32[768]{0:T(1024)S(1)} %convolution_reduce_fusion) | copy-start | bytes 9220
  117.8 59.6 %copy-start.44 = (f32[768]{0:T(1024)S(1)}, f32[768]{0:T(1024)}, u32[]{:S(2)}) copy-start(f32[768]{0:T(1024)} %param.42) | copy-start | bytes 9220
  175.9 4.9 %copy-start.46 = (f32[256]{0:T(256)}, f32[256]{0:T(256)S(1)}, u32[]{:S(2)}) copy-start(f32[256]{0:T(256)S(1)} %broadcast_multiply_fusion.5) | copy-start | bytes 3076
  177.3 3.6 copy-start.55
  177.3 3.5 copy-start.51
  177.3 5.0 %copy-start.60 = (pred[256]{0:T(512)(128)(4,1)S(1)}, pred[256]{0:T(512)(128)(4,1)}, u32[]{:S(2)}) copy-start(pred[256]{0:T(512)(128)(4,1)} %iota_compare_fusion.1) | copy-start | bytes 772
  187.8 3.9 copy-start.35
  187.8 3.9 copy-start.38
  212.0 6.4 %copy-start.6 = (f32[256,768]{1,0:T(8,128)S(1)}, f32[256,768]{1,0:T(8,128)}, u32[]{:S(2)}) copy-start(f32[256,768]{1,0:T(8,128)} %copy-done.5) | copy-start | bytes 2359300
  212.0 6.4 %copy-start.43 = (f32[768]{0:T(1024)S(1)}, f32[768]{0:T(1024)}, u32[]{:S(2)}) copy-start(f32[768]{0:T(1024)} %param.43) | copy-start | bytes 9220
  212.0 6.4 %copy-start.49 = (f32[256]{0:T(256)S(1)}, f32[256]{0:T(256)}, u32[]{:S(2)}) copy-start(f32[256]{0:T(256)} %copy-done.48) | copy-start | bytes 3076
  212.0 6.4 %copy-start.59 = (f32[256]{0:T(256)S(1)}, f32[256]{0:T(256)}, u32[]{:S(2)}) copy-start(f32[256]{0:T(256)} %fusion.251) | copy-start | bytes 3076
  218.4 3.8 copy-start.71
  222.2 2.2 copy-start.58
  222.2 3.5 copy-start.61
  224.4 1.5 copy-start.18
  224.4 3.0 copy-start.11
  230.5 1.7 copy-start.8
  230.5 1.7 copy-start.16
  235.6 3.0 copy-start.72
  238.6 1.4 copy-start.56
  238.6 1.8 copy-start.54
  238.6 1.8 copy-start.62
  240.0 3.4 copy-start.67
  240.0 4.2 copy-start.14
  244.2 3.6 copy-start.63
  244.2 3.6 copy-start.69
  244.2 3.6 copy-start.70
  460.8 2.2 copy-start.3
  463.0 5.9 %copy-start.7 = (f32[256,768]{1,0:T(8,128)S(1)}, f32[256,768]{1,0:T(8,128)}, u32[]{:S(2)}) copy-start(f32[256,768]{1,0:T(8,128)} %copy-done.5) | copy-start | bytes 2359300
  463.0 5.9 %copy-start.15 = (bf16[256,3072]{1,0:T(8,128)(2,1)S(1)}, bf16[256,3072]{1,0:T(8,128)(2,1)}, u32[]{:S(2)}) copy-start(bf16[256,3072]{1,0:T(8,128)(2,1)} %get-tuple-element.60) | copy-start | bytes 4718596
  468.8 4.6 copy-start.17
  473.5 1.7 copy-start.23
  473.5 2.5 copy-start.42
  473.5 3.1 copy-start.41
  473.5 3.7 copy-start.40
  473.5 4.3 copy-start.39
  473.5 5.0 %copy-start.21 = (f32[128,2048]{1,0:T(8,128)S(1)}, f32[128,2048]{1,0:T(8,128)}, u32[]{:S(2)}) copy-start(f32[128,2048]{1,0:T(8,128)} %get-tuple-element.127) | copy-start | bytes 3145732
  475.2 4.3 copy-start.20
  475.2 5.2 %copy-start.31 = (f32[72,768]{1,0:T(8,128)S(1)}, f32[72,768]{1,0:T(8,128)}, u32[]{:S(2)}) copy-start(f32[72,768]{1,0:T(8,128)} %get-tuple-element.43) | copy-start | bytes 663556
  475.9 5.2 %copy-start.36 = (f32[24,768]{1,0:T(8,128)S(1)}, f32[24,768]{1,0:T(8,128)}, u32[]{:S(2)}) copy-start(f32[24,768]{1,0:T(8,128)} %get-tuple-element.44) | copy-start | bytes 221188
  476.5 5.2 %copy-start.25 = (f32[96,768]{1,0:T(8,128)S(1)}, f32[96,768]{1,0:T(8,128)}, u32[]{:S(2)}) copy-start(f32[96,768]{1,0:T(8,128)} %get-tuple-element.45) | copy-start | bytes 884740
  478.4 4.0 copy-start.24
  (15 other events, 14.8 us)
Sparse Core Ops, SparseCore 0:
  9.6 49.0 all-gather.5
  60.3 30.7 all-gather.7
  92.6 17.4 all-gather.9
  111.5 37.4 all-gather.11
  150.4 37.4 all-gather.13

commit v3 on v2

--- a/solution.py
+++ b/solution.py
@@ -154,7 +154,7 @@
             held = self.part(stream, own_bit(*axis_bit))
         if stage == len(order) - 1 and entry["out"] is not None:
             total = land[...].astype(jnp.float32) + held[...].astype(jnp.float32)
-            rows = pl.ds(entry["start"], entry["rows"])
+            rows = pl.ds(entry["base"] + entry["start"], entry["rows"])
             if entry["fetch"]:
                 self.outputs[entry["out"]][rows] = total * entry["scale"]
             else:
@@ -280,6 +280,7 @@
         "order": order,
         "span": [d for d in dims if d in order],
         "fetch": fetch,
+        "base": 0,
         "scale": scale,
     }
 
@@ -379,7 +380,11 @@
     )(pixels)
 
 
-def unturn_kernel(in_ref, out_ref, lines):
+def unturn_kernel(blocks, heights, *refs):
+    in_ref, weight_ref, whole_ref, out_ref = refs[:4]
+    weight_out = refs[4 : 4 + len(heights)]
+    wide_out = refs[4 + len(heights) : -1]
+    lines = refs[-1]
     bands = out_ref.shape[1]
     halves, rows = lines.shape[:2]
     for half in range(halves):
@@ -391,19 +396,42 @@
             piece = lines[half, pl.ds(band, rows // bands, stride=bands), :]
             out_ref[0, band, pl.ds(half * 128, 128), :] = piece.T.astype(out_ref.dtype)
 
-
-def unturn_pixels(blocks, shape):
-    owners, images, share, slot = blocks.shape
+    @pl.when(pl.program_id(0) == 0)
+    def _():
+        base = 0
+        for number, height in enumerate(heights):
+            part = weight_ref[pl.ds(base, height), :]
+            weight_out[number][...] = part.T if number < len(heights) - 1 else part
+            base += height
+        unpack_blocks(blocks, whole_ref, wide_out, len(whole_ref.shape) - 2)
+
+
+def unturn_pixels(pixel_blocks, shape, weight_sums, heights, whole, wide_shapes):
+    owners, images, share, slot = pixel_blocks.shape
     bands, pixel_count = shape[1], shape[3]
+    model_dim = weight_sums.shape[1]
+    blocks = wide_plan(wide_shapes, math.prod(whole.shape[:-2]))[0]
+
+    def fixed(array_shape):
+        return pl.BlockSpec(array_shape, lambda i: (0,) * len(array_shape))
+
+    given = [(model_dim, height) for height in heights[:-1]] + [(heights[-1], model_dim)]
+    given += wide_shapes
     return pl.pallas_call(
-        unturn_kernel,
+        functools.partial(unturn_kernel, blocks, heights),
         grid=(images,),
-        out_shape=jax.ShapeDtypeStruct(shape, blocks.dtype),
-        in_specs=[pl.BlockSpec((owners, 1, share, slot), lambda i: (0, i, 0, 0))],
-        out_specs=pl.BlockSpec((1, bands, slot, pixel_count), lambda i: (i, 0, 0, 0)),
+        out_shape=[jax.ShapeDtypeStruct(shape, pixel_blocks.dtype)]
+        + [jax.ShapeDtypeStruct(s, jnp.float32) for s in given],
+        in_specs=[
+            pl.BlockSpec((owners, 1, share, slot), lambda i: (0, i, 0, 0)),
+            fixed(weight_sums.shape),
+            fixed(whole.shape),
+        ],
+        out_specs=[pl.BlockSpec((1, bands, slot, pixel_count), lambda i: (i, 0, 0, 0))]
+        + [fixed(s) for s in given],
         scratch_shapes=[pltpu.VMEM((slot // 128, pixel_count * bands, 128), jnp.float32)],
-        compiler_params=pltpu.CompilerParams(vmem_limit_bytes=20 << 20),
-    )(blocks)
+        compiler_params=pltpu.CompilerParams(vmem_limit_bytes=40 << 20),
+    )(pixel_blocks, weight_sums, whole)
 
 
 def at_band(place):
@@ -620,14 +648,15 @@
     params = take(8)
     gen_b_grad, gain_lines = take(2)
     (pixel_land,) = take(1)
-    outputs = take(bulk + 1)
-    wide_out = take(8)
+    outputs = take(2)
+    (whole,) = take(1)
     gen_ref, pix_ref, kern_ref, gath, stage_ref, part_ref, part_in, wide_ref = take(8)
-    expand_ref, shrink_ref = wide_out[4:6]
+    expand_ref, shrink_ref = take(2)
     own = take(2)
     landing = [take(len(stream["order"])) for stream in streams]
-    packed, whole = take(2)
-    load_sem, near_send, far_send, relay_send, block_recv, part_send, part_recv = take(7)
+    (packed,) = take(1)
+    load_sem, near_send, far_send, relay_send, onward_send = take(5)
+    block_recv, part_send, part_recv = take(3)
     send_sem, recv_sem, own_sem, gather_send, gather_recv = take(5)
     pixel_send, pixel_recv, pixel_own = take(3)
     sum_in, sum_send, sum_recv, share_send, share_recv, out_buffer, out_sem = take(7)
@@ -671,14 +700,23 @@
         )
 
     near = block_copy(low_ref, mine, beside, near_send)
-    far = [
-        block_copy(
-            low_ref, mine, lax.rem(place + step, depth) * 2 + side, far_send.at[step - 1]
-        )
-        for step in range(1, depth)
-    ]
-    for copy in far[:1] + [near] + far[1:]:
-        copy.start()
+    has_right, has_left = place + 1 < depth, place > 0
+
+    def to_right():
+        return block_copy(low_ref, mine, mine + 2, far_send.at[0])
+
+    def to_left():
+        return block_copy(low_ref, mine, mine - 2, far_send.at[1])
+
+    @pl.when(has_right)
+    def _():
+        to_right().start()
+
+    @pl.when(has_left)
+    def _():
+        to_left().start()
+
+    near.start()
     bits = (2,) * len(tok_dims)
     segments = gen_ref.reshape(bits + (gen_ref.shape[0] * model_dim >> len(bits), gen_ref.shape[2]))
     sums = Sums(
@@ -702,16 +740,30 @@
     gath[mine] = low_ref[...]
     loads[0].wait()
     make_kernels(gen_ref, even_ref, odd_ref, kern_ref, factor)
-    for stream in heavy:
-        sums.advance(stream, 0)
-        if stream + 2 < len(heavy):
-            sums.fetch(stream + 2)
     loads[1].wait()
     width = 256
 
+    def pair_at(step):
+        number = step - 1
+        left, right = place, depth - 1 - place
+        both = jnp.minimum(left, right)
+        turn = jnp.where(lax.rem(number, 2) == 0, -1, 1) * (lax.div(number, 2) + 1)
+        rest = jnp.where(right > left, 1, -1) * (number - both + 1)
+        offset = jnp.where(number < 2 * both, turn, rest)
+        return jnp.where(step == 0, place, place + offset)
+
     def relay(step):
-        block = lax.rem(place + step, depth) * 2 + side
+        block = pair_at(step) * 2 + side
         return block_copy(gath.at[block], block, beside, relay_send.at[step - 1])
+
+    def onward(step, act):
+        pair = pair_at(step)
+        block = pair * 2 + side
+        ahead = jnp.where(pair < place, mine + 2, mine - 2)
+
+        @pl.when(jnp.where(pair < place, place + 1 < depth, place > 0))
+        def _():
+            act(block_copy(gath.at[block], block, ahead, onward_send.at[step - 1]))
 
     def pixel_copy(image, step):
         target = lax.rem(mine + step, owners)
@@ -773,39 +825,60 @@
             def _(step):
                 pixel_copy(pair * 2 + parity, step).start()
 
+    done = 0
+    for step in range(1, depth):
+        block_copy(low_ref, pair_at(step) * 2 + side, beside, near_send).wait_recv()
+        onward(step, lambda copy: copy.start())
+        relay(step).start()
+        until = len(heavy) if step >= depth - 2 else len(heavy) * step // (depth - 2)
+        for stream in heavy[done:until]:
+            sums.advance(stream, 0)
+            if stream + 2 < len(heavy):
+                sums.fetch(stream + 2)
+        done = max(done, until)
+    hyper_dim = feature_ref.shape[1]
+    bands = feature_ref.shape[0]
+    first_row = lax.broadcasted_iota(jnp.int32, (8, hyper_dim), 0) == 0
+    tokens = jnp.concatenate(
+        [feature_ref[...], jnp.where(first_row, token_ref[...], 0.0)], axis=0
+    )
+    wide_width = 512
+    attention = tuple(params[number][...] for number in (0, 1, 2, 3, 6))
+    segment, segment_back = jax.vjp(
+        lambda t, p: hyper_attention(t, p, 1), tokens, attention
+    )
+    loads[2].wait()
+    loads[3].wait()
+    hyper_wide(segment, expand_ref, shrink_ref, wide_ref, wide_width)
+    norm_back = jax.vjp(
+        lambda v, g: layer_norm(v, g, EPS_HYPER), wide_ref[...], params[7][...]
+    )[1]
+
     @pl.loop(0, depth)
     def _(step):
-        pair = lax.rem(place + depth - step, depth)
-
-        @pl.when(step > 0)
+        pair = pair_at(step)
+
+        @pl.when(step == depth - 1)
         def _():
-            block_copy(low_ref, pair * 2 + side, beside, near_send).wait_recv()
-            relay(depth - step).start()
+            pixel_send_pair(place)
 
         block_copy(low_ref, pair * 2 + 1 - side, beside, near_send).wait_recv()
         pair_work(pair)
 
-    def pair_at(step):
-        return lax.rem(place + depth - step, depth)
-
-    waiting = [pair_at(step) for step in range(depth)]
-    pixel_send_pair(waiting.pop(0))
+    waiting = [pair_at(step) for step in range(1, depth)]
     part_ref[...] = jnp.zeros_like(part_ref)
+
+    def dk_rows(duo, parity):
+        return dk_ref[:, duo, parity].reshape(depth * owners * 8, model_dim)
 
     @pl.loop(0, dk_ref.shape[1])
     def _(duo):
         for parity in range(2):
-            rows = dk_ref[:, duo, parity].reshape(depth * owners * 8, model_dim)
             part_ref[parity] += jnp.dot(
-                rows, gen_ref[duo * 2 + parity], preferred_element_type=jnp.float32
+                dk_rows(duo, parity),
+                gen_ref[duo * 2 + parity],
+                preferred_element_type=jnp.float32,
             ).reshape(depth, owners * 8, -1)
-            weight = lax.dot_general(
-                rows,
-                (even_ref, odd_ref)[parity][...],
-                (((0,), (0,)), ((), ())),
-                preferred_element_type=jnp.float32,
-            )
-            gen_ref[duo * 2 + parity] = weight.astype(gen_ref.dtype)
 
     part_ref[...] = part_ref[...] * factor
 
@@ -823,6 +896,18 @@
     copies = [part_copy(step) for step in range(1, owners)]
     for copy in copies:
         copy.start()
+
+    @pl.loop(0, dk_ref.shape[1])
+    def _(duo):
+        for parity in range(2):
+            weight = lax.dot_general(
+                dk_rows(duo, parity),
+                (even_ref, odd_ref)[parity][...],
+                (((0,), (0,)), ((), ())),
+                preferred_element_type=jnp.float32,
+            )
+            gen_ref[duo * 2 + parity] = weight.astype(gen_ref.dtype)
+
     for stream in slices:
         sums.begin(stream)
     early = len(heavy) // 2
@@ -834,7 +919,7 @@
         total += part_in[step]
     pixel_send_pair(waiting.pop(0))
     rows = total.shape[1]
-    bands = rows // 2
+    half = jnp.where(side == 0, 0.0, 1.0)
     even_part = total[0].reshape(owners, 8, -1)
     odd_part = total[1].reshape(owners, 8, -1)
     low_rows = even_part + pltpu.roll(odd_part, 4, 1)
@@ -846,27 +931,11 @@
         + lax.rem(lax.broadcasted_iota(jnp.int32, (bands, rows), 0), 4)
     ).astype(jnp.float32)
     d_band = precise_dot(chooser, low_rows)
-    hyper_dim = d_band.shape[1]
-    first_row = lax.broadcasted_iota(jnp.int32, (8, hyper_dim), 0) == 0
-    tokens = jnp.concatenate(
-        [feature_ref[...], jnp.where(first_row, token_ref[...], 0.0)], axis=0
-    )
     cotangent = jnp.concatenate(
         [d_band, jnp.where(first_row, bias_grad_ref[...], 0.0)], axis=0
     )
-    width = 512
-    attention = tuple(params[place][...] for place in (0, 1, 2, 3, 6))
-    segment, segment_back = jax.vjp(
-        lambda t, p: hyper_attention(t, p, 1), tokens, attention
-    )
-    loads[2].wait()
-    loads[3].wait()
-    hyper_wide(segment, expand_ref, shrink_ref, wide_ref, width)
-    norm_back = jax.vjp(
-        lambda v, g: layer_norm(v, g, EPS_HYPER), wide_ref[...], params[7][...]
-    )[1]
     d_total, second_grad = norm_back(cotangent)
-    hyper_wide_back(segment, d_total, expand_ref, shrink_ref, wide_ref, width)
+    hyper_wide_back(segment, d_total, expand_ref, shrink_ref, wide_ref, wide_width)
     token_grad, param_grads = segment_back(wide_ref[...])
     small = [param_grads[0], param_grads[1], param_grads[2], param_grads[3]]
     line_row = lax.broadcasted_iota(jnp.int32, gain_lines.shape, 0)
@@ -952,7 +1021,6 @@
         spread.finish()
     for copy in moves + shares:
         copy.wait_send()
-    unpack_blocks(blocks, whole, wide_out, stages)
 
     @pl.loop(0, depth * 2)
     def _(image):
@@ -970,8 +1038,19 @@
                 device_id_type=MESH,
             ).wait()
 
-    for copy in copies + [near] + far + [relay(step) for step in range(1, depth)]:
+    for copy in copies + [near] + [relay(step) for step in range(1, depth)]:
         copy.wait_send()
+    for step in range(1, depth):
+        onward(step, lambda copy: copy.wait_send())
+
+    @pl.when(has_right)
+    def _():
+        to_right().wait_send()
+
+    @pl.when(has_left)
+    def _():
+        to_left().wait_send()
+
     sums.drain()
 
 
@@ -1000,22 +1079,24 @@
     rows = owners * 8
     split, outs, landing, streams = [], [], [], []
     order = halving_order(0, band_bits, tok_bits)
-    tallest = 0
+    tallest, base = 0, 0
     for k, weight in enumerate(weights):
         height = weight.shape[0] >> everything
         split.append(weight.reshape((2,) * everything + (height, weight.shape[1])))
-        outs.append(jax.ShapeDtypeStruct((height, weight.shape[1]), jnp.float32))
         for start, size in row_chunks(height, 2 if height > 32 else 1):
-            streams.append(stream_entry(k, k, start, size, order, dims, True))
+            streams.append(stream_entry(k, 0, start, size, order, dims, True))
+            streams[-1]["base"] = base
             landing += landing_shapes(streams[-1], weight.shape[1])
             tallest = max(tallest, size)
+        base += height
+    outs.append(jax.ShapeDtypeStruct((base, model_dim), jnp.float32))
     bulk = len(weights)
     tok_order = halving_order(2, band_bits, tok_bits)
     height = pixel_share * model_dim >> tok_bits
     outs.append(jax.ShapeDtypeStruct((height, hyper_dim), jnp.float32))
     for start, size in row_chunks(height, 4):
         out_rows = size
-        streams.append(stream_entry(bulk, bulk, start, size, tok_order, dims, False, factor))
+        streams.append(stream_entry(bulk, 1, start, size, tok_order, dims, False, factor))
         landing += landing_shapes(streams[-1], hyper_dim)
     wide_shapes = [p.shape for p in params[:6]] + [gen_b_grad.shape, gain_lines.shape]
     blocks, used, piece = wide_plan(wide_shapes, 1 << everything)
@@ -1035,15 +1116,17 @@
         functools.partial(tail_kernel, factor, plan),
         out_shape=[jax.ShapeDtypeStruct(pix.shape, low)]
         + outs
-        + [jax.ShapeDtypeStruct(shape, jnp.float32) for shape in wide_shapes],
+        + [jax.ShapeDtypeStruct(space, low)],
         in_specs=[pl.BlockSpec(memory_space=pl.ANY)] * (2 + bulk)
         + [pl.BlockSpec(memory_space=pltpu.VMEM)] * 10
         + [pl.BlockSpec(memory_space=pl.ANY)] * 2
         + [pl.BlockSpec(memory_space=pltpu.VMEM)] * 4,
         out_specs=[pl.BlockSpec(memory_space=pl.ANY)]
-        + [pl.BlockSpec(memory_space=pltpu.VMEM)] * bulk
-        + [pl.BlockSpec(memory_space=pl.ANY)]
-        + [pl.BlockSpec(memory_space=pltpu.VMEM)] * len(wide_shapes),
+        + [
+            pl.BlockSpec(memory_space=pltpu.VMEM),
+            pl.BlockSpec(memory_space=pl.ANY),
+            pl.BlockSpec(memory_space=pltpu.VMEM),
+        ],
         scratch_shapes=[
             pltpu.VMEM(gen_grid.shape, low),
             pltpu.VMEM(pix.shape, low),
@@ -1053,15 +1136,17 @@
             pltpu.VMEM((2, depth, rows, hyper_dim), jnp.float32),
             pltpu.VMEM((owners - 1, 2, rows, hyper_dim), jnp.float32),
             pltpu.VMEM((features.shape[0] + 8, hyper_dim), jnp.float32),
+            pltpu.VMEM(params[4].shape, jnp.float32),
+            pltpu.VMEM(params[5].shape, jnp.float32),
             own,
             own,
         ]
         + landing
         + [
             pltpu.VMEM(space, low),
-            pltpu.VMEM(space, low),
             dma((4,)),
             dma,
+            dma((2,)),
             dma((depth - 1,)),
             dma((depth - 1,)),
             dma((owners,)),
@@ -1116,7 +1201,7 @@
 
 
 def exact_gelu(values):
-    return jax.nn.gelu(values, approximate=False)
+    return 0.5 * values * (1.0 + lax.erf(values * math.sqrt(0.5)))
 
 
 def wave_features(lengths, model_dim):
@@ -1513,22 +1598,7 @@
     fill = -(3 + 2 * gain_rows) % 16
     gain_lines.append(jnp.zeros((fill, hyper_dim), jnp.float32))
     if paired:
-        (
-            grad_blocks,
-            qkv_sum,
-            out_sum,
-            up_sum,
-            down_sum,
-            grad_gen_w,
-            query_sum,
-            key_sum,
-            value_sum,
-            mix_sum,
-            expand_sum,
-            shrink_sum,
-            gen_b_sum,
-            line_sum,
-        ) = tail_call(
+        grad_blocks, weight_sums, grad_gen_w, whole = tail_call(
             gen_grid,
             pixel_lined,
             d_embed_low.reshape(slot_count, model_dim),
@@ -1553,7 +1623,31 @@
             factor,
             2,
         )
-        pixel_grad = unturn_pixels(grad_blocks, pixels.shape[1:])[None]
+        devices = owners * lax.axis_size("tok")
+        (
+            pixel_grad,
+            qkv_sum,
+            out_sum,
+            up_sum,
+            down_sum,
+            query_sum,
+            key_sum,
+            value_sum,
+            mix_sum,
+            expand_sum,
+            shrink_sum,
+            gen_b_sum,
+            line_sum,
+        ) = unturn_pixels(
+            grad_blocks,
+            pixels.shape[1:],
+            weight_sums,
+            [term.shape[0] // devices for term in weight_terms],
+            whole,
+            [part.shape for part in hyper_params[1:7]]
+            + [gen_b.shape, (3 + 2 * gain_rows + fill, hyper_dim)],
+        )
+        pixel_grad = pixel_grad[None]
     else:
         d_gathered = lax.all_gather(d_embed_low, "band", axis=0, tiled=True)
         grad_slices = jnp.einsum(
@@ -1624,6 +1718,7 @@
             ],
             3,
         )
+        qkv_sum, out_sum, up_sum = qkv_sum.T, out_sum.T, up_sum.T
     devices = owners * lax.axis_size("tok")
     place = band_place * lax.axis_size("tok") + lax.axis_index("tok")
     gain_share = model_dim // devices
@@ -1645,9 +1740,9 @@
         shrink_sum,
         line_sum[1],
         line_sum[2],
-        qkv_sum.T,
-        out_sum.T,
-        up_sum.T,
+        qkv_sum,
+        out_sum,
+        up_sum,
         down_sum,
         own_gain(line_sum[3 : 3 + gain_rows]),
         own_gain(line_sum[3 + gain_rows : 3 + 2 * gain_rows]),

time: 499 us -> 462 us (0.926)
  Pallas kernels: 275 us -> 256 us
  matrix products: 89 us -> 75.2 us
    pallas_call x1, Pallas kernels: 210 us -> 190 us  [tail_call(): pl.pallas_call(functools.partial(tail_kernel, factor, plan), out_shape=[j...]
    dot_general x1, matrix products: 20.1 us -> 6.45 us  [block_forward(): hidden = jnp.dot(normed_two, w_up_full, preferred_element_type=jnp.float32)]
    unnamed x161 -> x133, local copies, waits for them, and re-layouts: 20.3 us -> 17.3 us
  transfers between devices with their start and end apart: 6 -> 6, of which waited for: 1 -> 1; matrix products, arithmetic and copies ran while one was open for 14% -> 12% of each run, Pallas kernels for 12% -> 13%
where the time goes in v3:
time: 462 us; the launch traced here: 453 us
  Pallas kernels  256 us (55%)
  matrix products  75.2 us (16%)
  waiting for transfers between devices  60.5 us (13%)
  local copies, waits for them, and re-layouts  25.5 us (6%)
  between operations  15.9 us (3%)
  other arithmetic  12.4 us (3%)
  starting transfers between devices  7.62 us (2%)
    pallas_call x1, Pallas kernels, tail_call(): pl.pallas_call(functools.partial(tail_kernel, factor, plan), out_shape=[j...  190 us
    all_to_all x1, waiting for transfers between devices, body(): lax.all_to_all(turn_pixels(pixels[0], owners), 'band', 0, 0, tiled=True)  57.4 us
    pallas_call x1, Pallas kernels, embed_parts(): pl.pallas_call(functools.partial(embed_kernel, factor), out_shape=jax.Sha...  56.8 us
    unnamed x133, local copies, waits for them, and re-layouts  17.3 us
    dot_general x2, matrix products, hyper_layer(): jnp.einsum('nsf,fe->nse', expanded, hyper_down, precision=PRECISE)  14.8 us
    dot_general x4, matrix products, contract_rows(): lax.dot_general(left_side, right_side, (((0,), (0,)), ((), ())), preferre...  11.9 us
    dot_general x4, matrix products, contract_cols(): lax.dot_general(left_side, right_side, (((1,), (1,)), ((), ())), preferre...  10.4 us
  transfers between devices with their start and end apart: 6, of which 1 were waited for; matrix products, arithmetic and copies ran while one was open for 12% of the time, Pallas kernels for 13%

profile of v3, /device:TPU:0, one launch (start us, length us, event | category | flops | bytes accessed | tf_op | source)
XLA Modules:
  0.0 452.9 jit_solution(460776339325153632)
XLA Ops:
  7.2 0.7 all-gather.6.cloned.1.call-update
  8.0 0.7 all-gather.8.cloned.1.call-update
  8.7 0.7 all-gather.10.cloned.1.call-update
  10.0 2.2 copy-done.2
  12.2 2.9 shard_map.357
  15.1 2.0 copy-done.1
  17.1 7.4 %all-to-all-start = ((bf16[8,8,128,256]{3,2,1,0:T(8,128)(2,1)}), bf16[8,8,128,256]{3,2,1,0:T(8,128)(2,1)}, u32[]{:S(2)}, u32[]{:S(2)}) async-start(bf16[8,8,128,256]{3,2,1,0:T(8,128)(2,1)} %copy-done.1), calls=%async_computation | async-start | bytes 8388608 | tf_op jit(solution)/shard_map/all_to_all | solution.py:1515
  24.6 0.5 all-gather.14.cloned.1.call-update
  25.3 0.5 multiply_sine_fusion
  27.9 1.4 fusion.316
  29.4 0.8 fusion.113
  30.3 1.1 fusion.317
  31.6 5.1 %fusion.117 = (u8[33,2048]{1,0:T(8,128)(4,1)S(1)}, u8[33,2048]{1,0:T(8,128)(4,1)S(1)}, u8[33,2048]{1,0:T(8,128)(4,1)S(1)}, f32[8,33,2048]{2,1,0:T(8,128)}) fusion(f32[128,2048]{1,0:T(8,128)S(1)} %copy-done.21, f32[8,33,128]{2,1,0:T(8,128)S(1)} %get-tuple-element.137, f32[128]{0:T(128)S(1)} %copy-done.57, f32[8,33]{1,0:T(8,128)S(1)} %add_rsqrt_fusion.1, ...), kind=kOutput, calls=%fused_computation.164 | convolution fusion | flops 841184256 | bytes 3551808 | tf_op jit(solution)/shard_map/nse,ef->nsf/dot_general | solution.py:1255
  38.2 0.6 pad.3.clone
  39.3 1.0 and_convert_fusion
  40.4 12.1 %fusion.318 = (f32[8,33]{1,0:T(8,128)S(1)}, f32[8,33,128]{2,1,0:T(8,128)S(1)}) fusion(f32[2048,128]{1,0:T(8,128)} %refs_17_.1, pred[8,33,2048]{2,1,0:T(8,128)(4,1)S(1)} %and_convert_fusion.2, pred[8,33,2048]{2,1,0:T(8,128)(4,1)S(1)} %get-tuple-element.158, pred[8,33,2048]{2,1,0:T(8,128)(4,1)S(1)} %get-tuple-element.157, ...), kind=kOutput, calls=%fused_computation.416 | convolution fusion | flops 863621888 | bytes 5107296 | tf_op jit(solution)/shard_map/nsf,fe->nse/dot_general | solution.py:1258
  52.8 0.7 rev.3
  55.9 0.7 fusion.236
  56.6 2.7 fusion.321
  60.4 57.4 %all-to-all-done.pix_hbm.refs_1_ = bf16[8,8,128,256]{3,2,1,0:T(8,128)(2,1)} async-done(((bf16[8,8,128,256]{3,2,1,0:T(8,128)(2,1)}), bf16[8,8,128,256]{3,2,1,0:T(8,128)(2,1)}, u32[]{:S(2)}, u32[]{:S(2)}) %all-to-all-start) | async-done | bytes 4194336 | tf_op jit(solution)/shard_map/all_to_all | solution.py:1515
  117.8 56.8 %shard_map.358 = f32[256,768]{1,0:T(8,128)} custom-call(bf16[32,768,128]{2,1,0:T(8,128)(2,1)} %bitcast.233, bf16[8,8,128,256]{3,2,1,0:T(8,128)(2,1)} %all-to-all-done.pix_hbm.refs_1_, bf16[256,128]{1,0:T(8,128)(2,1)} %bitcast.214, bf16[256,128]{1,0:T(8,128)(2,1)} %bitcast.219), custom_call_target="tpu_custom_call" | custom-call | flops 10000000000 | bytes 120000000 | tf_op jit(solution)/shard_map/pallas_call | solution.py:604
  174.6 1.3 add_reduce_fusion
  175.9 1.4 multiply_reduce_fusion.6
  177.4 3.5 convolution_convert_fusion.3
  180.9 1.6 copy.95
  182.4 1.9 fusion.322
  184.9 0.6 copy-done.32
  185.5 2.4 fusion.92
  188.0 2.2 fusion.323
  190.2 0.8 copy-done.7
  191.3 0.6 fusion.245
  191.9 6.5 %multiply_convert_fusion.1 = (bf16[256,3072]{1,0:T(8,128)(2,1)}, f32[256,3072]{1,0:T(8,128)}) fusion(bf16[768,3072]{1,0:T(8,128)(2,1)} %all-gather.12.cloned.1.call-done, f32[256,768]{1,0:T(8,128)} %copy-done.7, f32[768]{0:T(1024)} %param.43, f32[256]{0:T(256)} %fusion.245, f32[256]{0:T(256)} %copy-done.35), kind=kOutput, calls=%fused_computation.9 | convolution fusion | flops 1212678144 | bytes 10228736 | tf_op jit(solution)/shard_map/dot_general | solution.py:1377
  198.4 5.6 %add_convert_fusion = bf16[256,3072]{1,0:T(8,128)(2,1)S(1)} fusion(f32[256,3072]{1,0:T(8,128)} %get-tuple-element.152, bf16[3072,768]{1,0:T(8,128)(2,1)} %all-gather.14.cloned.1.call-done, bf16[1,1,256,768]{3,2,1,0:T(8,128)(2,1)} %param.26, pred[256]{0:T(512)(128)(4,1)} %iota_compare_fusion.1), kind=kOutput, calls=%fused_computation.7 | convolution fusion | flops 1218772992 | bytes 9830656 | tf_op jit(solution)/shard_map/dot_general | solution.py:1337
  204.1 3.8 convolution_convert_fusion.1
  207.9 2.2 multiply_reduce_fusion.1
  210.5 0.9 copy-done.12
  211.6 1.5 convolution_convert_fusion.4
  213.1 1.2 convolution_convert_fusion.5
  214.3 1.9 copy.97
  216.3 1.7 fusion.102
  218.0 0.8 multiply_reduce_fusion
  218.9 0.9 multiply_convert_fusion
  219.7 0.6 fusion.100
  220.9 0.5 copy-done.6
  221.5 3.0 convolution_convert_fusion.2
  224.5 1.3 multiply_reduce_fusion.2
  226.3 0.7 copy-done.13
  227.1 1.0 fusion.313
  228.1 0.9 fusion.324.refs_11_
  229.1 0.8 broadcast_multiply_fusion.refs_20_
  229.9 3.6 convolution_convert_fusion
  233.5 0.7 maximum_maximum_fusion.refs_21_
  234.2 189.9 %shard_map.359 = (bf16[8,8,128,256]{3,2,1,0:T(8,128)(2,1)}, f32[288,768]{1,0:T(8,128)}, f32[6144,128]{1,0:T(8,128)}, bf16[2,2,2,2,2,176,128]{6,5,4,3,2,1,0:T(8,128)(2,1)}) custom-call(bf16[32,768,128]{2,1,0:T(8,128)(2,1)} %bitcast.234, bf16[8,8,128,256]{3,2,1,0:T(8,128)(2,1)} %all-to-all-done.pix_hbm.refs_1_, bf16[2,2,2,2,2,72,768]{6,5,4,3,2,1,0:T(8,128)(2,1)} %bitcast.192, ...), custom_call_target="tpu_custom_call" | custom-call | flops 20000000000 | bytes 300000000 | tf_op jit(solution)/shard_map/pallas_call | solution.py:1115
  424.1 2.2 copy-done.3
  426.3 1.4 copy-done.4
  427.6 1.2 copy-done.5
  428.8 6.2 %shard_map.360 = (bf16[8,4,256,256]{3,2,1,0:T(8,128)(2,1)}, f32[768,72]{1,0:T(8,128)S(1)}, f32[768,24]{1,0:T(8,128)S(1)}, f32[768,96]{1,0:T(8,128)S(1)}, f32[96,...) custom-call(bf16[8,8,128,256]{3,2,1,0:T(8,128)(2,1)S(1)} %copy-done., ...), custom_call_target="tpu_custom_call" | custom-call | tf_op jit(solution)/shard_map/pallas_call | solution.py:420
  435.5 0.6 dynamic_slice.11
  436.1 0.6 dynamic_slice.10
  436.7 0.8 copy.102
  437.4 0.8 copy.101
  438.3 0.9 copy.103
  439.2 5.1 %fusion.99 = bf16[1,1,256,768]{3,2,1,0:T(8,128)(2,1)} fusion(f32[256,768]{1,0:T(8,128)S(1)} %copy-done.9, bf16[256,3072]{1,0:T(8,128)(2,1)} %get-tuple-element.151, bf16[3072,768]{1,0:T(8,128)(2,1)} %all-gather.14.cloned.1.call-done, pred[256]{0:T(512)(128)(4,1)S(1)} %copy-done.53), kind=kOutput, calls=%fused_computation.129 | convolution fusion | flops 1208549376 | bytes 7471360 | tf_op jit(solution)/shard_map/dot_general | solution.py:1379
  444.2 1.7 copy.129
  (189 shorter events, 11.4 us)
Async XLA Ops:
  7.2 52.4 %copy-start = (f32[128,768]{1,0:T(8,128)S(1)}, f32[128,768]{1,0:T(8,128)}, u32[]{:S(2)}) copy-start(f32[128,768]{1,0:T(8,128)} %param.28) | copy-start | bytes 1179652
  7.2 110.6 %all-gather.6.cloned.1.call-start = ((), (), s32[]{:S(2)}) async-start(), calls=%async_computation.1 | async-start | bytes 7864320 | tf_op jit(solution)/shard_map/all_gather | solution.py:1523
  7.9 169.4 %all-gather.8.cloned.1.call-start = ((), (), s32[]{:S(2)}) async-start(), calls=%async_computation.2 | async-start | bytes 4423680 | tf_op jit(solution)/shard_map/all_gather | solution.py:1526
  8.7 179.3 %all-gather.10.cloned.1.call-start = ((), (), s32[]{:S(2)}) async-start(), calls=%async_computation.3 | async-start | bytes 1474560 | tf_op jit(solution)/shard_map/all_gather | solution.py:1527
  9.4 182.5 %all-gather.12.cloned.1.call-start = ((), (), s32[]{:S(2)}) async-start(), calls=%async_computation.4 | async-start | bytes 5898240 | tf_op jit(solution)/shard_map/all_gather | solution.py:1528
  10.0 2.2 copy-start.2
  15.1 2.0 copy-start.1
  17.1 8.1 %copy-start.55 = (s32[1,8,32]{2,1,0:T(8,128)S(1)}, s32[1,8,32]{2,1,0:T(8,128)}, u32[]{:S(2)}) copy-start(s32[1,8,32]{2,1,0:T(8,128)} %param.24) | copy-start | bytes 3076
  17.1 8.1 %copy-start.59 = (f32[64]{0:T(128)S(1)}, f32[64]{0:T(128)}, u32[]{:S(2)}) copy-start(f32[64]{0:T(128)} %param.23) | copy-start | bytes 772
  17.1 8.8 %copy-start.42 = (f32[128]{0:T(128)S(1)}, f32[128]{0:T(128)}, u32[]{:S(2)}) copy-start(f32[128]{0:T(128)} %param.29) | copy-start | bytes 1540
  17.1 8.9 %copy-start.26 = (f32[128,128]{1,0:T(8,128)S(1)}, f32[128,128]{1,0:T(8,128)}, u32[]{:S(2)}) copy-start(f32[128,128]{1,0:T(8,128)} %refs_12_.1) | copy-start | bytes 196612
  17.1 9.3 %copy-start.27 = (f32[128,128]{1,0:T(8,128)S(1)}, f32[128,128]{1,0:T(8,128)}, u32[]{:S(2)}) copy-start(f32[128,128]{1,0:T(8,128)} %refs_13_.1) | copy-start | bytes 196612
  17.1 100.7 %all-to-all-start = ((bf16[8,8,128,256]{3,2,1,0:T(8,128)(2,1)}), bf16[8,8,128,256]{3,2,1,0:T(8,128)(2,1)}, u32[]{:S(2)}, u32[]{:S(2)}) async-start(bf16[8,8,128,256]{3,2,1,0:T(8,128)(2,1)} %copy-done.1), calls=%async_computation | async-start | bytes 8388608 | tf_op jit(solution)/shard_map/all_to_all | solution.py:1515
  24.5 2.3 copy-start.25
  24.5 173.9 %all-gather.14.cloned.1.call-start = ((), (), s32[]{:S(2)}) async-start(), calls=%async_computation.5 | async-start | bytes 5898240 | tf_op jit(solution)/shard_map/all_gather | solution.py:1529
  27.9 2.4 copy-start.23
  29.3 2.3 copy-start.21
  29.3 2.3 copy-start.57
  40.3 12.3 %copy-start.56 = (f32[128]{0:T(128)S(1)}, f32[128]{0:T(128)}, u32[]{:S(2)}) copy-start(f32[128]{0:T(128)} %param.37) | copy-start | bytes 1540
  52.8 6.5 %copy-start.24 = (bf16[4,2,8,4,128]{4,3,1,2,0:T(4,128)(2,1)}, bf16[4,2,8,4,128]{4,3,1,2,0:T(4,128)(2,1)S(1)}, u32[]{:S(2)}) copy-start(bf16[4,2,8,4,128]{4,3,1,2,0:T(4,128)(2,1)S(1)} %copy.126) | copy-start | bytes 196612
  54.1 5.2 %copy-start.22 = (f32[1,32,128]{2,1,0:T(8,128)}, f32[1,32,128]{2,1,0:T(8,128)S(1)}, u32[]{:S(2)}) copy-start(f32[1,32,128]{2,1,0:T(8,128)S(1)} %fusion.240) | copy-start | bytes 49156
  59.9 128.1 %copy-start.28 = (f32[768]{0:T(1024)}, f32[768]{0:T(1024)S(1)}, u32[]{:S(2)}) copy-start(f32[768]{0:T(1024)S(1)} %convolution_reduce_fusion) | copy-start | bytes 9220
  117.8 59.5 %copy-start.37 = (f32[768]{0:T(1024)S(1)}, f32[768]{0:T(1024)}, u32[]{:S(2)}) copy-start(f32[768]{0:T(1024)} %param.42) | copy-start | bytes 9220
  175.9 4.9 %copy-start.39 = (f32[256]{0:T(256)}, f32[256]{0:T(256)S(1)}, u32[]{:S(2)}) copy-start(f32[256]{0:T(256)S(1)} %broadcast_multiply_fusion.5) | copy-start | bytes 3076
  177.3 3.6 copy-start.47
  177.3 3.6 copy-start.43
  177.3 5.1 %copy-start.51 = (pred[256]{0:T(512)(128)(4,1)S(1)}, pred[256]{0:T(512)(128)(4,1)}, u32[]{:S(2)}) copy-start(pred[256]{0:T(512)(128)(4,1)} %iota_compare_fusion.1) | copy-start | bytes 772
  188.0 3.9 copy-start.31
  188.0 3.9 copy-start.33
  190.2 1.1 copy-start.35
  198.4 5.7 %copy-start.8 = (f32[256,768]{1,0:T(8,128)S(1)}, f32[256,768]{1,0:T(8,128)}, u32[]{:S(2)}) copy-start(f32[256,768]{1,0:T(8,128)} %copy-done.7) | copy-start | bytes 2359300
  198.4 5.7 %copy-start.34 = (f32[768]{0:T(1024)S(1)}, f32[768]{0:T(1024)}, u32[]{:S(2)}) copy-start(f32[768]{0:T(1024)} %param.43) | copy-start | bytes 9220
  198.4 5.7 %copy-start.36 = (f32[256]{0:T(256)S(1)}, f32[256]{0:T(256)}, u32[]{:S(2)}) copy-start(f32[256]{0:T(256)} %copy-done.35) | copy-start | bytes 3076
  198.4 5.7 %copy-start.41 = (f32[256]{0:T(256)S(1)}, f32[256]{0:T(256)}, u32[]{:S(2)}) copy-start(f32[256]{0:T(256)} %fusion.245) | copy-start | bytes 3076
  204.1 3.8 copy-start.14
  207.9 2.2 copy-start.50
  207.9 3.4 copy-start.52
  210.1 1.3 copy-start.16
  210.1 1.5 copy-start.20
  210.1 3.0 copy-start.15
  210.5 0.9 copy-start.12
  216.3 1.7 copy-start.11
  216.3 1.7 copy-start.18
  220.3 1.1 copy-start.6
  220.3 1.1 copy-start.29
  220.4 1.1 copy-start.38
  220.4 1.1 copy-start.40
  220.4 1.1 copy-start.44
  221.5 3.0 copy-start.62
  224.5 1.4 copy-start.48
  224.5 1.8 copy-start.46
  224.5 1.8 copy-start.53
  225.9 1.1 copy-start.13
  225.9 1.2 copy-start.17
  225.9 3.2 copy-start.58
  225.9 4.0 copy-start.10
  229.9 3.6 copy-start.54
  229.9 3.6 copy-start.60
  229.9 3.6 copy-start.61
  424.1 2.2 copy-start.3
  426.3 1.4 copy-start.4
  427.6 1.2 copy-start.5
  428.8 10.4 %copy-start.9 = (f32[256,768]{1,0:T(8,128)S(1)}, f32[256,768]{1,0:T(8,128)}, u32[]{:S(2)}) copy-start(f32[256,768]{1,0:T(8,128)} %copy-done.7) | copy-start | bytes 2359300
  439.2 5.1 %copy-start.19 = (f32[6144,128]{1,0:T(8,128)S(1)}, f32[6144,128]{1,0:T(8,128)}, u32[]{:S(2)}) copy-start(f32[6144,128]{1,0:T(8,128)} %get-tuple-element.182) | copy-start | bytes 9437188
  (5 other events, 3.5 us)
Sparse Core Ops, SparseCore 0:
  9.6 49.0 all-gather.5
  60.3 30.8 all-gather.7
  92.7 17.4 all-gather.9
  111.6 37.4 all-gather.11
  150.5 37.4 all-gather.13
